TPU v7x, 32 devices: a whole 2x2x4 slice. The times are simulated.
32 devices in a mesh: fsdp: 4 (over z), expert: 8 (over y, x, core).
Axes of the slice: x: 2, y: 2, z: 4, core: 2. Of those that a mesh axis runs over, the one named last changes fastest.
Arguments:
- residual_in: bfloat16 [4, 1024, 1536], P('fsdp', 'expert'), may hold values from -30 to 30
- cotangent: bfloat16 [4, 1024, 1536], P('fsdp', 'expert'), may hold values from -30 to 30
- gain_attn: bfloat16 [1536], P('fsdp'), may hold values from 0.5 to 1.5
- w_query: bfloat16 [1536, 1536], P('fsdp'), may hold values from -0.5 to 0.5
- w_key: bfloat16 [1536, 512], P('fsdp'), may hold values from -0.5 to 0.5
- w_value: bfloat16 [1536, 512], P('fsdp'), may hold values from -0.625 to 0.625
- w_out: bfloat16 [1536, 1536], P(None, 'fsdp'), may hold values from -1.5 to 1.5
- gain_ffn: bfloat16 [1536], P('fsdp'), may hold values from 0.5 to 1.5
- w_router: bfloat16 [1536, 24], P('fsdp'), may hold values from -0.078125 to 0.078125
- w_gate: bfloat16 [24, 1536, 512], P('expert'), may hold values from -0.15625 to 0.15625
- w_up: bfloat16 [24, 1536, 512], P('expert'), may hold values from -0.15625 to 0.15625
- w_down: bfloat16 [24, 512, 1536], P('expert'), may hold values from -4 to 4
- route_ids: int32 [4, 1024, 8], P('fsdp', 'expert'), may hold values from 0 to 23, all different within a row; in each aligned block of 128 rows (0 to 127, 128 to 255, ..., all dimensions but the last counted through in order) at most 64 rows name the same one
Outputs:
- output: bfloat16 [4, 1024, 1536], P('fsdp', 'expert')
- input_grad: bfloat16 [4, 1024, 1536], P('fsdp', 'expert')
- grad_gain_attn: float32 [1536], P('fsdp')
- grad_query: float32 [1536, 1536], P('fsdp')
- grad_key: float32 [1536, 512], P('fsdp')
- grad_value: float32 [1536, 512], P('fsdp')
- grad_out_proj: float32 [1536, 1536], P(None, 'fsdp')
- grad_gain_ffn: float32 [1536], P('fsdp')
- grad_router: float32 [1536, 24], P('fsdp')
- grad_gate: float32 [24, 1536, 512], P('expert', 'fsdp')
- grad_up: float32 [24, 1536, 512], P('expert', 'fsdp')
- grad_down: float32 [24, 512, 1536], P('expert', None, 'fsdp')
- residual_rms: float32 [5], replicated
Inputs may be any that keep to these rules, and one draw needn't show every extreme that they name: `route_ids`: each token names 8 different experts; within the 128 tokens of one device (aligned blocks of the flattened sequences) no expert is named more than 64 times, a bound that some block reaches.
All inputs are finite; a program needn't handle non-finite values.
Results may differ from a plain program's by a relative error of at most 0.024.
Values may be sent and summed in bfloat16 or wider, within the bound.
A program may use at most 256 MiB of HBM per device.

v0:
```python
import jax
import jax.numpy as jnp
from jax import lax
from jax.sharding import PartitionSpec as P

HEAD_DIM = 64
BLOCK = 256


EPSILON = 1e-06
RESIDUAL_SCALE = 0.22
ATTENTION_SCALE = 0.015625
ROPE_BASE = 10000.0
MASKED = -1e30
HIGHEST = lax.Precision.HIGHEST


def rotated(values, positions, direction):
    half_dim = HEAD_DIM // 2
    exponent = jnp.arange(half_dim, dtype=jnp.float32) * (2.0 / HEAD_DIM)
    angles = positions.astype(jnp.float32)[:, None] * jnp.power(ROPE_BASE, -exponent)[None, :]
    cosine = jnp.cos(angles)[:, None, :]
    sine_term = direction * jnp.sin(angles)[:, None, :]
    first_half = values[..., :half_dim]
    second = values[..., half_dim:]
    return jnp.concatenate(
        [first_half * cosine - second * sine_term, second * cosine + first_half * sine_term],
        axis=-1,
    )


def norm_back(grad_normed, normed, inverse):
    return inverse * (grad_normed - normed * jnp.mean(grad_normed * normed, axis=-1, keepdims=True))


def per_device(
    residual_in,
    cotangent,
    gain_attn,
    w_query,
    w_key,
    w_value,
    w_out,
    gain_ffn,
    w_router,
    w_gate,
    w_up,
    w_down,
    route_ids,
):
    tokens = residual_in.shape[1]
    model_width = residual_in.shape[2]
    groups = w_key.shape[1] // HEAD_DIM
    per_group = w_query.shape[1] // w_key.shape[1]
    experts_here = w_gate.shape[0]
    experts_all = w_router.shape[1]
    peer_count = lax.axis_size("expert")
    top_count = route_ids.shape[2]
    capacity = (3 * tokens * top_count // (2 * experts_all) + 7) // 8 * 8
    gain_one, query_full, key_full, value_full, out_full, gain_two, router_full = (
        lax.all_gather(gain_attn, "fsdp", axis=0, tiled=True),
        lax.all_gather(w_query, "fsdp", axis=0, tiled=True),
        lax.all_gather(w_key, "fsdp", axis=0, tiled=True),
        lax.all_gather(w_value, "fsdp", axis=0, tiled=True),
        lax.all_gather(w_out, "fsdp", axis=1, tiled=True),
        lax.all_gather(gain_ffn, "fsdp", axis=0, tiled=True),
        lax.all_gather(w_router, "fsdp", axis=0, tiled=True),
    )
    gain_one = gain_one.astype(jnp.float32)
    gain_two = gain_two.astype(jnp.float32)
    token_rows = residual_in[0].astype(jnp.float32)
    inverse_one = lax.rsqrt(jnp.mean(token_rows * token_rows, axis=-1, keepdims=True) + EPSILON)
    normed_one = token_rows * inverse_one
    attn_in = (normed_one * gain_one).astype(jnp.bfloat16)
    query_pre = jnp.dot(attn_in, query_full, preferred_element_type=jnp.float32)
    key_pre = jnp.dot(attn_in, key_full, preferred_element_type=jnp.float32)
    value_pre = jnp.dot(attn_in, value_full, preferred_element_type=jnp.float32)
    position = lax.axis_index("expert") * tokens + jnp.arange(tokens, dtype=jnp.int32)
    queries = rotated(query_pre.reshape(tokens, -1, HEAD_DIM), position, 1.0).astype(jnp.bfloat16)
    key_rows = (
        rotated(key_pre.reshape(tokens, groups, HEAD_DIM), position, 1.0)
        .astype(jnp.bfloat16)
        .reshape(tokens, groups * HEAD_DIM)
    )
    value_rows = value_pre.astype(jnp.bfloat16)
    all_keys, all_values = (
        lax.all_gather(key_rows, "expert", axis=0, tiled=True),
        lax.all_gather(value_rows, "expert", axis=0, tiled=True),
    )
    length = all_keys.shape[0]
    key_blocks = jnp.arange(length, dtype=jnp.int32) // BLOCK
    allowed = key_blocks[None, :] <= (position // BLOCK)[:, None]
    query_heads = queries.reshape(tokens, groups, per_group * HEAD_DIM).transpose(1, 0, 2)
    key_heads = all_keys.reshape(length, groups, HEAD_DIM).transpose(1, 0, 2)
    value_heads = all_values.reshape(length, groups, HEAD_DIM).transpose(1, 0, 2)

    def scores_of(query_group, key_group):
        query_split = query_group.reshape(tokens, per_group, HEAD_DIM)
        raw_scores = (
            jnp.einsum("tgd,kd->gtk", query_split, key_group, preferred_element_type=jnp.float32)
            * ATTENTION_SCALE
        )
        return jnp.where(allowed[None], raw_scores, MASKED)

    def attend_forward(operands):
        query_group, key_group, value_group = operands
        scores = scores_of(query_group, key_group)
        row_peak = jnp.max(scores, axis=-1, keepdims=True)
        lifted = jnp.exp(scores - row_peak)
        row_total = jnp.sum(lifted, axis=-1, keepdims=True)
        weights = (lifted / row_total).astype(jnp.bfloat16)
        mixture = jnp.einsum(
            "gtk,kd->tgd", weights, value_group, preferred_element_type=jnp.float32
        )
        return (
            mixture.reshape(tokens, per_group * HEAD_DIM),
            (row_peak + jnp.log(row_total))[..., 0],
        )

    head_out, log_sums = lax.map(attend_forward, (query_heads, key_heads, value_heads))
    attended = head_out.transpose(1, 0, 2).reshape(tokens, -1).astype(jnp.bfloat16)
    branch = jnp.dot(attended, out_full, preferred_element_type=jnp.float32)
    middle = token_rows + RESIDUAL_SCALE * branch
    inverse_two = lax.rsqrt(jnp.mean(middle * middle, axis=-1, keepdims=True) + EPSILON)
    normed_two = middle * inverse_two
    routed = (normed_two * gain_two).astype(jnp.bfloat16)
    logits = jnp.dot(routed, router_full, preferred_element_type=jnp.float32)
    route_rows = route_ids[0]
    picker = (
        route_rows[:, :, None] == jnp.arange(experts_all, dtype=jnp.int32)[None, None, :]
    ).astype(jnp.float32)
    chosen = jnp.sum(picker * logits[:, None, :], axis=-1)
    gate_probs = jax.nn.softmax(chosen, axis=-1)
    flat_ids = route_rows.reshape(-1)
    onehot = (flat_ids[:, None] == jnp.arange(experts_all, dtype=jnp.int32)[None, :]).astype(
        jnp.int32
    )
    slot_index = jnp.sum((jnp.cumsum(onehot, axis=0) - onehot) * onehot, axis=1)
    source_token = jnp.arange(tokens * top_count, dtype=jnp.int32) // top_count
    outgoing = (
        jnp.zeros((experts_all, capacity, model_width), jnp.bfloat16)
        .at[flat_ids, slot_index]
        .set(routed[source_token])
    )
    received = lax.all_to_all(
        outgoing.reshape(peer_count, experts_here, capacity, model_width),
        "expert",
        split_axis=0,
        concat_axis=0,
        tiled=True,
    )
    gate_pre = jnp.einsum("sjcd,jdf->sjcf", received, w_gate, preferred_element_type=jnp.float32)
    up_pre = jnp.einsum("sjcd,jdf->sjcf", received, w_up, preferred_element_type=jnp.float32)
    sigmoid_gate = jax.nn.sigmoid(gate_pre)
    silu_gate = gate_pre * sigmoid_gate
    hidden = (silu_gate * up_pre).astype(jnp.bfloat16)
    produced = jnp.einsum(
        "sjcf,jfd->sjcd", hidden, w_down, preferred_element_type=jnp.float32
    ).astype(jnp.bfloat16)
    returned = lax.all_to_all(produced, "expert", split_axis=0, concat_axis=0, tiled=True).reshape(
        experts_all, capacity, model_width
    )
    picked = (
        returned[flat_ids, slot_index].reshape(tokens, top_count, model_width).astype(jnp.float32)
    )
    expert_sum = jnp.einsum("tk,tkd->td", gate_probs, picked, precision=HIGHEST)
    outcome = middle + RESIDUAL_SCALE * expert_sum
    grad_rows = cotangent[0].astype(jnp.float32)
    grad_expert_sum = RESIDUAL_SCALE * grad_rows
    grad_probs = jnp.einsum("td,tkd->tk", grad_expert_sum, picked, precision=HIGHEST)
    grad_picked = (
        (gate_probs[:, :, None] * grad_expert_sum[:, None, :])
        .astype(jnp.bfloat16)
        .reshape(tokens * top_count, model_width)
    )
    outgoing_grad = (
        jnp.zeros((experts_all, capacity, model_width), jnp.bfloat16)
        .at[flat_ids, slot_index]
        .set(grad_picked)
    )
    grad_produced = lax.all_to_all(
        outgoing_grad.reshape(peer_count, experts_here, capacity, model_width),
        "expert",
        split_axis=0,
        concat_axis=0,
        tiled=True,
    )
    grad_hidden = jnp.einsum(
        "sjcd,jfd->sjcf", grad_produced, w_down, preferred_element_type=jnp.float32
    )
    grad_w_down = jnp.einsum(
        "sjcf,sjcd->jfd", hidden, grad_produced, preferred_element_type=jnp.float32
    )
    grad_gate_pre = (
        grad_hidden * up_pre * sigmoid_gate * (1.0 + gate_pre * (1.0 - sigmoid_gate))
    ).astype(jnp.bfloat16)
    grad_up_pre = (grad_hidden * silu_gate).astype(jnp.bfloat16)
    grad_w_gate = jnp.einsum(
        "sjcd,sjcf->jdf", received, grad_gate_pre, preferred_element_type=jnp.float32
    )
    grad_w_up = jnp.einsum(
        "sjcd,sjcf->jdf", received, grad_up_pre, preferred_element_type=jnp.float32
    )
    grad_received = (
        jnp.einsum("sjcf,jdf->sjcd", grad_gate_pre, w_gate, preferred_element_type=jnp.float32)
        + jnp.einsum("sjcf,jdf->sjcd", grad_up_pre, w_up, preferred_element_type=jnp.float32)
    ).astype(jnp.bfloat16)
    grad_returned = lax.all_to_all(
        grad_received, "expert", split_axis=0, concat_axis=0, tiled=True
    ).reshape(experts_all, capacity, model_width)
    grad_copies = (
        grad_returned[flat_ids, slot_index]
        .astype(jnp.float32)
        .reshape(tokens, top_count, model_width)
    )
    grad_chosen = gate_probs * (
        grad_probs - jnp.sum(gate_probs * grad_probs, axis=-1, keepdims=True)
    )
    grad_logits = jnp.einsum("tk,tke->te", grad_chosen, picker, precision=HIGHEST).astype(
        jnp.bfloat16
    )
    grad_router = jnp.einsum("td,te->de", routed, grad_logits, preferred_element_type=jnp.float32)
    grad_routed = jnp.einsum(
        "te,de->td", grad_logits, router_full, preferred_element_type=jnp.float32
    ) + jnp.sum(grad_copies, axis=1)
    grad_gain_two = jnp.sum(grad_routed * normed_two, axis=0)
    grad_middle = grad_rows + norm_back(grad_routed * gain_two, normed_two, inverse_two)
    grad_branch = (RESIDUAL_SCALE * grad_middle).astype(jnp.bfloat16)
    grad_out_proj = jnp.einsum(
        "ta,td->ad", attended, grad_branch, preferred_element_type=jnp.float32
    )
    grad_attended = jnp.einsum(
        "td,ad->ta", grad_branch, out_full, preferred_element_type=jnp.float32
    ).astype(jnp.bfloat16)
    grad_heads = grad_attended.reshape(tokens, groups, per_group * HEAD_DIM).transpose(1, 0, 2)

    def attend_back(operands):
        query_group, key_group, value_group, log_sum, grad_group = operands
        scores = scores_of(query_group, key_group)
        probs = jnp.exp(scores - log_sum[..., None])
        grad_split = grad_group.reshape(tokens, per_group, HEAD_DIM)
        grad_value_group = jnp.einsum(
            "gtk,tgd->kd",
            probs.astype(jnp.bfloat16),
            grad_split,
            preferred_element_type=jnp.float32,
        )
        grad_weights = jnp.einsum(
            "tgd,kd->gtk", grad_split, value_group, preferred_element_type=jnp.float32
        )
        grad_scores = (
            probs * (grad_weights - jnp.sum(probs * grad_weights, axis=-1, keepdims=True))
        ).astype(jnp.bfloat16)
        grad_query_group = (
            jnp.einsum("gtk,kd->tgd", grad_scores, key_group, preferred_element_type=jnp.float32)
            * ATTENTION_SCALE
        )
        grad_key_group = (
            jnp.einsum(
                "gtk,tgd->kd",
                grad_scores,
                query_group.reshape(tokens, per_group, HEAD_DIM),
                preferred_element_type=jnp.float32,
            )
            * ATTENTION_SCALE
        )
        return (
            grad_query_group.reshape(tokens, per_group * HEAD_DIM),
            grad_key_group,
            grad_value_group,
        )

    grad_query_heads, grad_key_heads, grad_value_heads = lax.map(
        attend_back, (query_heads, key_heads, value_heads, log_sums, grad_heads)
    )
    own_key_grad, own_value_grad = (
        lax.psum_scatter(
            grad_key_heads.astype(jnp.bfloat16), "expert", scatter_dimension=1, tiled=True
        ).astype(jnp.float32),
        lax.psum_scatter(
            grad_value_heads.astype(jnp.bfloat16), "expert", scatter_dimension=1, tiled=True
        ).astype(jnp.float32),
    )
    grad_key_pre = (
        rotated(own_key_grad.transpose(1, 0, 2), position, -1.0)
        .astype(jnp.bfloat16)
        .reshape(tokens, -1)
    )
    grad_value_pre = own_value_grad.transpose(1, 0, 2).reshape(tokens, -1).astype(jnp.bfloat16)
    grad_query_rot = grad_query_heads.transpose(1, 0, 2).reshape(tokens, -1, HEAD_DIM)
    grad_query_pre = (
        rotated(grad_query_rot, position, -1.0).astype(jnp.bfloat16).reshape(tokens, -1)
    )
    grad_attn_in = (
        jnp.einsum("ta,da->td", grad_query_pre, query_full, preferred_element_type=jnp.float32)
        + jnp.einsum("ta,da->td", grad_key_pre, key_full, preferred_element_type=jnp.float32)
        + jnp.einsum("ta,da->td", grad_value_pre, value_full, preferred_element_type=jnp.float32)
    )
    grad_w_query = jnp.einsum(
        "td,ta->da", attn_in, grad_query_pre, preferred_element_type=jnp.float32
    )
    grad_w_key = jnp.einsum("td,ta->da", attn_in, grad_key_pre, preferred_element_type=jnp.float32)
    grad_w_value = jnp.einsum(
        "td,ta->da", attn_in, grad_value_pre, preferred_element_type=jnp.float32
    )
    grad_gain_one = jnp.sum(grad_attn_in * normed_one, axis=0)
    grad_input = grad_middle + norm_back(grad_attn_in * gain_one, normed_one, inverse_one)
    square_parts = jnp.stack(
        [
            jnp.sum(token_rows * token_rows),
            jnp.sum(middle * middle),
            jnp.sum(outcome * outcome),
            jnp.sum(grad_middle * grad_middle),
            jnp.sum(grad_input * grad_input),
        ]
    )
    square_totals = lax.psum(square_parts, ("fsdp", "expert"))
    entry_count = tokens * model_width * lax.axis_size("fsdp") * lax.axis_size("expert")
    root_means = jnp.sqrt(square_totals / entry_count)
    reduced = (
        lax.psum_scatter(
            grad_gain_one.astype(jnp.bfloat16), "fsdp", scatter_dimension=0, tiled=True
        ).astype(jnp.float32),
        lax.psum_scatter(
            grad_w_query.astype(jnp.bfloat16), "fsdp", scatter_dimension=0, tiled=True
        ).astype(jnp.float32),
        lax.psum_scatter(
            grad_w_key.astype(jnp.bfloat16), "fsdp", scatter_dimension=0, tiled=True
        ).astype(jnp.float32),
        lax.psum_scatter(
            grad_w_value.astype(jnp.bfloat16), "fsdp", scatter_dimension=0, tiled=True
        ).astype(jnp.float32),
        lax.psum_scatter(
            grad_out_proj.astype(jnp.bfloat16), "fsdp", scatter_dimension=1, tiled=True
        ).astype(jnp.float32),
        lax.psum_scatter(
            grad_gain_two.astype(jnp.bfloat16), "fsdp", scatter_dimension=0, tiled=True
        ).astype(jnp.float32),
        lax.psum_scatter(
            grad_router.astype(jnp.bfloat16), "fsdp", scatter_dimension=0, tiled=True
        ).astype(jnp.float32),
        lax.psum_scatter(
            grad_w_gate.astype(jnp.bfloat16), "fsdp", scatter_dimension=1, tiled=True
        ).astype(jnp.float32),
        lax.psum_scatter(
            grad_w_up.astype(jnp.bfloat16), "fsdp", scatter_dimension=1, tiled=True
        ).astype(jnp.float32),
        lax.psum_scatter(
            grad_w_down.astype(jnp.bfloat16), "fsdp", scatter_dimension=2, tiled=True
        ).astype(jnp.float32),
    )
    summed = (
        lax.psum(reduced[0].astype(jnp.bfloat16), "expert").astype(jnp.float32),
        lax.psum(reduced[1].astype(jnp.bfloat16), "expert").astype(jnp.float32),
        lax.psum(reduced[2].astype(jnp.bfloat16), "expert").astype(jnp.float32),
        lax.psum(reduced[3].astype(jnp.bfloat16), "expert").astype(jnp.float32),
        lax.psum(reduced[4].astype(jnp.bfloat16), "expert").astype(jnp.float32),
        lax.psum(reduced[5].astype(jnp.bfloat16), "expert").astype(jnp.float32),
        lax.psum(reduced[6].astype(jnp.bfloat16), "expert").astype(jnp.float32),
    )
    expert_parts = (reduced[7], reduced[8], reduced[9])
    return (
        outcome.astype(jnp.bfloat16)[None],
        grad_input.astype(jnp.bfloat16)[None],
        summed[0],
        summed[1],
        summed[2],
        summed[3],
        summed[4],
        summed[5],
        summed[6],
        expert_parts[0],
        expert_parts[1],
        expert_parts[2],
        root_means,
    )


def solution(mesh):
    in_specs = (
        P("fsdp", "expert", None),
        P("fsdp", "expert", None),
        P("fsdp"),
        P("fsdp", None),
        P("fsdp", None),
        P("fsdp", None),
        P(None, "fsdp"),
        P("fsdp"),
        P("fsdp", None),
        P("expert", None, None),
        P("expert", None, None),
        P("expert", None, None),
        P("fsdp", "expert", None),
    )
    out_specs = (
        P("fsdp", "expert", None),
        P("fsdp", "expert", None),
        P("fsdp"),
        P("fsdp", None),
        P("fsdp", None),
        P("fsdp", None),
        P(None, "fsdp"),
        P("fsdp"),
        P("fsdp", None),
        P("expert", "fsdp", None),
        P("expert", "fsdp", None),
        P("expert", None, "fsdp"),
        P(),
    )
    return jax.shard_map(
        per_device, mesh=mesh, in_specs=in_specs, out_specs=out_specs, check_vma=False
    )
```

profile of v0, /device:TPU:0, one launch (start us, length us, event | category | flops | bytes accessed | tf_op | source)
XLA Modules:
  0.0 1456.4 jit_solution(14906248372527690927)
XLA Ops:
  9.4 13.6 all-gather
  24.2 25.1 %all-gather.9.cloned.1.call-done = bf16[1536,512]{1,0:T(8,128)(2,1)} async-done(((bf16[384,512]{1,0:T(8,128)(2,1)}), bf16[1536,512]{1,0:T(8,128)(2,1)}) %all-gather.9.cloned.1.call-update) | async-done | bytes 1572880 | tf_op jit(solution)/shard_map/all_gather | solution.py:64
  49.3 2.6 convolution_convert_fusion.6
  53.4 33.4 %all-gather.13.cloned.1.call-done = bf16[1536,512]{1,0:T(8,128)(2,1)} async-done(((bf16[384,512]{1,0:T(8,128)(2,1)}), bf16[1536,512]{1,0:T(8,128)(2,1)}) %all-gather.13.cloned.1.call-update) | async-done | bytes 1572880 | tf_op jit(solution)/shard_map/all_gather | solution.py:63
  91.1 11.9 all-gather.1
  103.1 6.8 reduce-window.6
  113.1 89.4 %all-gather.17.cloned.1.call-done = bf16[1536,1536]{1,0:T(8,128)(2,1)} async-done(((bf16[384,1536]{1,0:T(8,128)(2,1)}), bf16[1536,1536]{1,0:T(8,128)(2,1)}) %all-gather.17.cloned.1.call-update) | async-done | bytes 4718608 | tf_op jit(solution)/shard_map/all_gather | solution.py:62
  202.5 6.7 copy.84
  209.3 3.9 fusion.97
  213.4 13.4 all-gather.15.cloned.1.call-done
  226.8 22.6 %while.30 = (s32[]{:T(128)}, bf16[8,128,192]{1,2,0:T(8,128)(2,1)S(1)}, f32[8,3,128]{2,1,0:T(4,128)}, bf16[8,1024,64]{1,2,0:T(8,128)(2,1)S(1)}, bf16[8,1024,64]{1...) while((s32[]{:T(128)}, ...), condition=%wide.region_4.5_spmd.clone.clone, body=%wide.region_1.4_spmd.clone.sunk.clone | while | flops 103939712 | bytes 5556337 | solution.py:120
  249.4 68.2 %all-gather.19.cloned.1.call-done = bf16[1536,1536]{1,0:T(8,128)(2,1)} async-done(((bf16[1536,384]{1,0:T(8,128)(2,1)}), bf16[1536,1536]{1,0:T(8,128)(2,1)}) %all-gather.19.cloned.1.call-update) | async-done | bytes 4718608 | tf_op jit(solution)/shard_map/all_gather | solution.py:65
  317.6 3.3 multiply_reduce_fusion.6
  322.0 19.1 %scatter_custom_fusion = bf16[1536,1536]{1,0:T(8,128)(2,1)} fusion(s32[1024]{0:T(1024)S(1)} %get-tuple-element.247, bf16[128,1536]{1,0:T(8,128)(2,1)S(1)} %multiply_convert_fusion.1, s32[1024]{0:T(1024)S(1)} %get-tuple-element.246, bf16[]{:T(256)} %constant.126.clone.1), kind=kCustom, calls=%fused_computation.100 | custom fusion | bytes 4718594
  341.1 59.0 %all_to_all.20 = bf16[8,3,64,1536]{3,2,1,0:T(8,128)(2,1)S(1)} all-to-all(bf16[8,3,64,1536]{3,2,1,0:T(8,128)(2,1)} %bitcast.428), channel_id=1, replica_groups=mesh['fsdp'=4,'expert'=8] {'expert'}, dimensions={0} | all-to-all | bytes 9437184 | tf_op jit(solution)/shard_map/all_to_all | solution.py:145
  400.2 6.3 fusion.39
  406.5 4.5 fusion.64
  411.1 2.8 convert_bitcast_fusion
  416.3 4.8 all-to-all-start.1
  421.1 13.4 all_gather.35
  436.7 39.1 %all-to-all-done.1 = bf16[8,3,64,1536]{3,2,1,0:T(8,128)(2,1)} async-done(((bf16[8,3,64,1536]{3,2,1,0:T(8,128)(2,1)}), bf16[8,3,64,1536]{3,2,1,0:T(8,128)(2,1)}, u32[]{:S(2)}, u32[]{:S(2)}) %all-to-all-start.1) | async-done | bytes 4718624 | tf_op jit(solution)/shard_map/all_to_all | solution.py:160
  475.8 17.8 %gather_fusion = bf16[1024,1536]{1,0:T(8,128)(2,1)S(1)} fusion(bf16[24,64,1536]{2,1,0:T(8,128)(2,1)} %bitcast.32, s32[1024]{0:T(1024)S(1)} %bitcast.421), kind=kCustom, calls=%fused_computation.1 | custom fusion | bytes 6299648 | tf_op jit(solution)/shard_map/gather | solution.py:164
  493.6 7.9 fusion.60
  507.9 9.5 scatter_custom_fusion.1
  517.3 58.9 %all_to_all.21 = bf16[8,3,64,1536]{3,2,1,0:T(8,128)(2,1)S(1)} all-to-all(bf16[8,3,64,1536]{3,2,1,0:T(8,128)(2,1)} %bitcast.427), channel_id=1, replica_groups=mesh['fsdp'=4,'expert'=8] {'expert'}, dimensions={0} | all-to-all | bytes 9437184 | tf_op jit(solution)/shard_map/all_to_all | solution.py:181
  576.2 8.6 fusion.59
  584.8 5.6 fusion.37
  590.4 6.7 fusion.51
  597.1 4.9 copy.95
  602.0 4.6 all-to-all-start.3
  611.5 4.4 fusion.62
  615.9 45.4 %all-to-all-done.3 = bf16[8,3,64,1536]{3,2,1,0:T(8,128)(2,1)} async-done(((bf16[8,3,64,1536]{3,2,1,0:T(8,128)(2,1)}), bf16[8,3,64,1536]{3,2,1,0:T(8,128)(2,1)}, u32[]{:S(2)}, u32[]{:S(2)}) %all-to-all-start.3) | async-done | bytes 4718624 | tf_op jit(solution)/shard_map/all_to_all | solution.py:208
  661.3 17.8 %gather_fusion.1 = bf16[1024,1536]{1,0:T(8,128)(2,1)S(1)} fusion(bf16[24,64,1536]{2,1,0:T(8,128)(2,1)} %bitcast.48, s32[1024]{0:T(1024)S(1)} %bitcast.422), kind=kCustom, calls=%fused_computation.2 | custom fusion | bytes 6299648 | tf_op jit(solution)/shard_map/gather | solution.py:212
  684.5 4.0 convolution_convert_fusion.4
  688.8 64.0 %while.31 = (s32[]{:T(128)}, f32[8,128,192]{1,2,0:T(8,128)S(1)}, bf16[8,1024,64]{1,2,0:T(8,128)(2,1)}, bf16[8,1024,64]{1,2,0:T(8,128)(2,1)}, bf16[8,1024,64]{1,2...) while((s32[]{:T(128)}, f32[8,128,192]{1,2,0:T(8,128)S(1)}, ...), condition=%wide.region_19.20_spmd.clone.clone, body=%wide.region_17.19_spmd.clone.sunk.clone | while | flops 255417984 | bytes 13676693 | solution.py:273
  753.6 2.6 copy.119
  758.4 2.6 copy.117
  763.4 4.5 convolution_convert_fusion
  767.9 6.7 copy.121
  774.7 16.4 %reduce-scatter.33.cloned.1.call-done = bf16[128,512]{1,0:T(8,128)(2,1)} async-done(((bf16[1024,512]{1,0:T(8,128)(2,1)}), bf16[128,512]{1,0:T(8,128)(2,1)}) %reduce-scatter.33.cloned.1.call-update) | async-done | bytes 131088
  794.4 36.5 %reduce-scatter.31.cloned.1.call-done = bf16[128,512]{1,0:T(8,128)(2,1)} async-done(((bf16[1024,512]{1,0:T(8,128)(2,1)}), bf16[128,512]{1,0:T(8,128)(2,1)}) %reduce-scatter.31.cloned.1.call-update) | async-done | bytes 131088
  834.4 3.6 convolution_convert_fusion.1
  840.2 7.7 bitcast_convert_fusion
  847.9 10.9 copy.125
  858.7 6.9 copy.129
  867.0 7.4 bitcast_convert_fusion.1
  875.8 7.3 bitcast_convert_fusion.2
  885.0 33.5 %reduce-scatter.35.cloned.1.call-done = bf16[384,1536]{1,0:T(8,128)(2,1)} async-done(((bf16[1536,1536]{1,0:T(8,128)(2,1)}), bf16[384,1536]{1,0:T(8,128)(2,1)}) %reduce-scatter.35.cloned.1.call-update) | async-done | bytes 1179664
  920.9 36.3 %reduce-scatter.25.cloned.1.call-done = bf16[384,512]{1,0:T(8,128)(2,1)} async-done(((bf16[1536,512]{1,0:T(8,128)(2,1)}), bf16[384,512]{1,0:T(8,128)(2,1)}) %reduce-scatter.25.cloned.1.call-update) | async-done | bytes 393232 | tf_op jit(solution)/shard_map/reduce_scatter | solution.py:330
  957.2 37.2 %reduce-scatter.23.cloned.1.call-done = bf16[384,512]{1,0:T(8,128)(2,1)} async-done(((bf16[1536,512]{1,0:T(8,128)(2,1)}), bf16[384,512]{1,0:T(8,128)(2,1)}) %reduce-scatter.23.cloned.1.call-update) | async-done | bytes 393232 | tf_op jit(solution)/shard_map/reduce_scatter | solution.py:327
  994.4 86.3 %reduce-scatter.21.cloned.1.call-done = bf16[384,1536]{1,0:T(8,128)(2,1)} async-done(((bf16[1536,1536]{1,0:T(8,128)(2,1)}), bf16[384,1536]{1,0:T(8,128)(2,1)}) %reduce-scatter.21.cloned.1.call-update) | async-done | bytes 1179664 | tf_op jit(solution)/shard_map/reduce_scatter | solution.py:324
  1080.8 4.1 fusion.132
  1088.6 3.4 stack.23
  1092.0 13.1 reduce-scatter.37.cloned.1.call-done
  1106.0 43.1 %psum.63 = f32[5]{0:T(128)S(1)} all-reduce(f32[5]{0:T(128)S(1)} %stack.23), channel_id=1, replica_groups=mesh['fsdp'=4,'expert'=8] {'fsdp','expert'}, use_global_device_ids=true, to_apply=%region_47.48 | all-reduce | flops 5 | bytes 40 | tf_op jit(solution)/shard_map/psum | solution.py:317
  1149.1 12.7 all-reduce.4
  1162.0 23.7 %all-reduce.2 = (bf16[384]{0:T(512)(128)(2,1)S(1)}, bf16[384]{0:T(512)(128)(2,1)S(1)}, bf16[384,24]{0,1:T(8,128)(2,1)S(1)}) all-reduce(bf16[384]{0:T(512)(128)(2,1)S(1)} %dynamic-slice.1, bf16[384]{0:T(512)(128)(2,1)S(1)} %dynamic-slice.3, bf16[384,24]{0,1:T(8,128)(2,1)S(1)} %copy.124), channel_id=1, replica_groups=mesh['fsdp'=4,'expert'=8] {'expert'}, use_global_device_ids=true, to_apply=%region_25.26 | all-reduce | flops 9984 | bytes 39936 | tf_op jit(solution)/shard_map/psum | solution.py:353
  1188.0 4.2 reduce-scatter.39.cloned.1.call-done
  1192.2 2.6 reshape.583
  1197.6 82.4 %reduce-scatter.29.cloned.1.call-done = bf16[3,384,512]{2,1,0:T(8,128)(2,1)} async-done(((bf16[3,1536,512]{2,1,0:T(8,128)(2,1)}), bf16[3,384,512]{2,1,0:T(8,128)(2,1)}) %reduce-scatter.29.cloned.1.call-update) | async-done | bytes 1179664 | tf_op jit(solution)/shard_map/reduce_scatter | solution.py:345
  1280.0 3.0 convert_element_type.320
  1283.0 85.0 %reduce-scatter.27.cloned.1.call-done = bf16[3,384,512]{2,1,0:T(8,128)(2,1)} async-done(((bf16[3,1536,512]{2,1,0:T(8,128)(2,1)}), bf16[3,384,512]{2,1,0:T(8,128)(2,1)}) %reduce-scatter.27.cloned.1.call-update) | async-done | bytes 1179664 | tf_op jit(solution)/shard_map/reduce_scatter | solution.py:342
  1368.0 3.0 convert_element_type.318
  1371.0 71.0 %all-reduce.7.cloned.1.call-done = (bf16[384,1536]{1,0:T(8,128)(2,1)}, bf16[384,512]{1,0:T(8,128)(2,1)}, bf16[384,512]{1,0:T(8,128)(2,1)}, bf16[1536,384]{1,0:T(8,128)(2,1)}) async-done(((bf16[384,1536]{1,0:T(8,128)(2,1)}, bf16[384,512]{1,0:T(8,128)(2,1)}, bf16[384,512]{1,0:T(8,128)(2,1)}, bf16[1536,384]{1,0:T(8,128)(2,1)}), (bf16[384,1536]{1,0:T(8,128)(2,1)}, bf16[384,512]{1,0:T(8,128)(2,1)}, ...) | async-done | bytes 3145744 | tf_op jit(solution)/shard_map/psum | solution.py:354
  (381 shorter events, 158.4 us)
Async XLA Ops:
  7.2 42.2 %all-gather.9.cloned.1.call-start = ((), (), s32[]{:S(2)}) async-start(), calls=%async_computation.14 | async-start | bytes 1966080 | tf_op jit(solution)/shard_map/all_gather | solution.py:64
  7.9 78.9 %all-gather.13.cloned.1.call-start = ((), (), s32[]{:S(2)}) async-start(), calls=%async_computation.16 | async-start | bytes 1966080 | tf_op jit(solution)/shard_map/all_gather | solution.py:63
  8.7 103.0 %all-gather.11.cloned.1.call-start = ((), (), s32[]{:S(2)}) async-start(), calls=%async_computation.15 | async-start | bytes 1179648 | tf_op jit(solution)/shard_map/all_gather | solution.py:88
  24.2 185.1 %copy-start.36 = (f32[128]{0:T(128)}, f32[128]{0:T(128)S(1)}, u32[]{:S(2)}) copy-start(f32[128]{0:T(128)S(1)} %add_rsqrt_fusion.1) | copy-start | bytes 1540
  24.2 64.4 %copy-start = (bf16[1,128,1536]{2,1,0:T(8,128)(2,1)S(1)}, bf16[1,128,1536]{2,1,0:T(8,128)(2,1)}, u32[]{:S(2)}) copy-start(bf16[1,128,1536]{2,1,0:T(8,128)(2,1)} %param.17) | copy-start | bytes 1179652
  52.0 150.6 %all-gather.17.cloned.1.call-start = ((), (), s32[]{:S(2)}) async-start(), calls=%async_computation.18 | async-start | bytes 5898240 | tf_op jit(solution)/shard_map/all_gather | solution.py:62
  52.6 174.2 %all-gather.15.cloned.1.call-start = ((), (), s32[]{:S(2)}) async-start(), calls=%async_computation.17 | async-start | bytes 1179648 | tf_op jit(solution)/shard_map/all_gather | solution.py:87
  53.4 159.8 %copy-start.25 = (f32[128,32]{0,1:T(8,128)}, f32[128,32]{0,1:T(8,128)S(1)}, u32[]{:S(2)}) copy-start(f32[128,32]{0,1:T(8,128)S(1)} %get-tuple-element.240) | copy-start | bytes 49156
  86.8 3.8 copy-start.35
  88.6 2.5 copy-start.43
  88.6 21.8 %copy-start.45 = (s32[2]{0:T(128)S(1)}, s32[2]{0:T(128)}, u32[]{:S(2)}) copy-start(s32[2]{0:T(128)} %constant.143) | copy-start | bytes 28
  88.6 21.9 %copy-start.44 = (s32[2]{0:T(128)S(1)}, s32[2]{0:T(128)}, u32[]{:S(2)}) copy-start(s32[2]{0:T(128)} %constant.140) | copy-start | bytes 28
  90.0 227.6 %all-gather.19.cloned.1.call-start = ((), (), s32[]{:S(2)}) async-start(), calls=%async_computation.19 | async-start | bytes 5898240 | tf_op jit(solution)/shard_map/all_gather | solution.py:65
  103.1 217.9 %copy-start.30 = (f32[1536]{0:T(1024)}, f32[1536]{0:T(1024)S(1)}, u32[]{:S(2)}) copy-start(f32[1536]{0:T(1024)S(1)} %reshape.551) | copy-start | bytes 18436
  110.6 211.4 %copy-start.42 = (s32[1024]{0:T(1024)}, s32[1024]{0:T(1024)S(1)}, u32[]{:S(2)}) copy-start(s32[1024]{0:T(1024)S(1)} %get-tuple-element.247) | copy-start | bytes 12292
  249.4 71.5 %copy-start.4 = (bf16[8,128,192]{1,2,0:T(8,128)(2,1)}, bf16[8,128,192]{1,2,0:T(8,128)(2,1)S(1)}, u32[]{:S(2)}) copy-start(bf16[8,128,192]{1,2,0:T(8,128)(2,1)S(1)} %get-tuple-element.105) | copy-start | bytes 1179652
  249.4 71.5 %copy-start.10 = (bf16[8,1024,64]{1,2,0:T(8,128)(2,1)}, bf16[8,1024,64]{1,2,0:T(8,128)(2,1)S(1)}, u32[]{:S(2)}) copy-start(bf16[8,1024,64]{1,2,0:T(8,128)(2,1)S(1)} %get-tuple-element.534) | copy-start | bytes 3145732
  249.4 71.5 %copy-start.11 = (bf16[8,128,192]{1,2,0:T(8,128)(2,1)}, bf16[8,128,192]{1,2,0:T(8,128)(2,1)S(1)}, u32[]{:S(2)}) copy-start(bf16[8,128,192]{1,2,0:T(8,128)(2,1)S(1)} %get-tuple-element.535) | copy-start | bytes 1179652
  249.4 71.5 %copy-start.33 = (s32[128]{0:T(128)}, s32[128]{0:T(128)S(1)}, u32[]{:S(2)}) copy-start(s32[128]{0:T(128)S(1)} %get-tuple-element.573) | copy-start | bytes 1540
  320.9 79.2 %copy-start.40 = (f32[128]{0:T(128)}, f32[128]{0:T(128)S(1)}, u32[]{:S(2)}) copy-start(f32[128]{0:T(128)S(1)} %add_rsqrt_fusion) | copy-start | bytes 1540
  322.0 113.9 %copy-start.7 = (bf16[128,1536]{1,0:T(8,128)(2,1)}, bf16[128,1536]{1,0:T(8,128)(2,1)S(1)}, u32[]{:S(2)}) copy-start(bf16[128,1536]{1,0:T(8,128)(2,1)S(1)} %multiply_convert_fusion.1) | copy-start | bytes 1179652
  341.1 65.4 %slice-start = ((s8[4718592]{0:T(1024)(128)(4,1)}), s8[4194304]{0:T(1024)(128)(4,1)S(1)}, s32[]{:S(2)}) async-start(s8[4718592]{0:T(1024)(128)(4,1)} %bitcast.442), calls=%async_computation.31 | async-start | bytes 8388608
  400.2 6.3 copy-start.5
  400.2 6.3 slice-start.1
  400.2 10.9 slice-start.2
  406.5 4.5 copy-start.48
  406.5 4.5 slice-start.3
  411.0 2.9 copy-start.47
  416.3 4.8 copy-start.38
  416.3 18.1 %copy-start.15 = (bf16[1,128,1536]{2,1,0:T(8,128)(2,1)S(1)}, bf16[1,128,1536]{2,1,0:T(8,128)(2,1)}, u32[]{:S(2)}) copy-start(bf16[1,128,1536]{2,1,0:T(8,128)(2,1)} %param.18) | copy-start | bytes 1179652
  416.3 59.5 %all-to-all-start.1 = ((bf16[8,3,64,1536]{3,2,1,0:T(8,128)(2,1)}), bf16[8,3,64,1536]{3,2,1,0:T(8,128)(2,1)}, u32[]{:S(2)}, u32[]{:S(2)}) async-start(bf16[8,3,64,1536]{3,2,1,0:T(8,128)(2,1)} %copy.92), calls=%async_computation.1 | async-start | bytes 9437184 | tf_op jit(solution)/shard_map/all_to_all | solution.py:160
  434.5 41.3 %copy-start.23 = (bf16[1536,24]{0,1:T(8,128)(2,1)}, bf16[1536,24]{0,1:T(8,128)(2,1)S(1)}, u32[]{:S(2)}) copy-start(bf16[1536,24]{0,1:T(8,128)(2,1)S(1)} %all_gather.35) | copy-start | bytes 221188
  436.1 39.7 %copy-start.32 = (f32[128,8]{0,1:T(8,128)}, f32[128,8]{0,1:T(8,128)S(1)}, u32[]{:S(2)}) copy-start(f32[128,8]{0,1:T(8,128)S(1)} %select_reduce_fusion.1) | copy-start | bytes 12292
  436.2 39.7 %copy-start.39 = (f32[128]{0:T(128)}, f32[128]{0:T(128)S(1)}, u32[]{:S(2)}) copy-start(f32[128]{0:T(128)S(1)} %reduce_max.18) | copy-start | bytes 1540
  517.3 58.9 %copy-start.49 = (f32[3,8,64,512]{3,2,1,0:T(8,128)S(1)}, f32[3,8,64,512]{3,2,1,0:T(8,128)}, u32[]{:S(2)}) copy-start(f32[3,8,64,512]{3,2,1,0:T(8,128)} %copy-done.48) | copy-start | bytes 9437188
  517.3 58.9 %copy-start.50 = (f32[3,8,64,512]{3,2,1,0:T(8,128)S(1)}, f32[3,8,64,512]{3,2,1,0:T(8,128)}, u32[]{:S(2)}) copy-start(f32[3,8,64,512]{3,2,1,0:T(8,128)} %get-tuple-element.244) | copy-start | bytes 9437188
  576.2 8.6 copy-start.6
  584.8 5.6 copy-start.13
  602.0 59.4 %all-to-all-start.3 = ((bf16[8,3,64,1536]{3,2,1,0:T(8,128)(2,1)}), bf16[8,3,64,1536]{3,2,1,0:T(8,128)(2,1)}, u32[]{:S(2)}, u32[]{:S(2)}) async-start(bf16[8,3,64,1536]{3,2,1,0:T(8,128)(2,1)} %copy.95), calls=%async_computation.3 | async-start | bytes 9437184 | tf_op jit(solution)/shard_map/all_to_all | solution.py:208
  606.6 184.5 %reduce-scatter.33.cloned.1.call-start = ((), (), s32[]{:S(2)}) async-start(), calls=%async_computation.26 | async-start | bytes 1179648
  679.1 2.4 copy-start.2
  679.2 2.4 copy-start.9
  679.2 2.4 copy-start.31
  679.2 2.4 copy-start.41
  684.5 4.3 copy-start.20
  684.5 4.3 copy-start.34
  758.4 72.5 %reduce-scatter.31.cloned.1.call-start = ((), (), s32[]{:S(2)}) async-start(), calls=%async_computation.25 | async-start | bytes 1179648
  763.1 155.4 %reduce-scatter.35.cloned.1.call-start = ((), (), s32[]{:S(2)}) async-start(), calls=%async_computation.27 | async-start | bytes 5898240
  774.6 17.8 %copy-start.37 = (f32[128]{0:T(128)S(1)}, f32[128]{0:T(128)}, u32[]{:S(2)}) copy-start(f32[128]{0:T(128)} %copy-done.36) | copy-start | bytes 1540
  774.7 57.6 %copy-start.26 = (f32[128,32]{0,1:T(8,128)S(1)}, f32[128,32]{0,1:T(8,128)}, u32[]{:S(2)}) copy-start(f32[128,32]{0,1:T(8,128)} %copy-done.25) | copy-start | bytes 49156
  774.7 57.6 %copy-start.29 = (f32[128,32]{0,1:T(8,128)S(1)}, f32[128,32]{0,1:T(8,128)}, u32[]{:S(2)}) copy-start(f32[128,32]{0,1:T(8,128)} %get-tuple-element.238) | copy-start | bytes 49156
  774.7 182.5 %reduce-scatter.25.cloned.1.call-start = ((), (), s32[]{:S(2)}) async-start(), calls=%async_computation.22 | async-start | bytes 1966080 | tf_op jit(solution)/shard_map/reduce_scatter | solution.py:330
  794.3 39.9 %copy-start.22 = (f32[8,128,192]{1,2,0:T(8,128)S(1)}, f32[8,128,192]{1,2,0:T(8,128)}, u32[]{:S(2)}) copy-start(f32[8,128,192]{1,2,0:T(8,128)} %copy-done.21) | copy-start | bytes 2359300
  794.3 200.1 %reduce-scatter.23.cloned.1.call-start = ((), (), s32[]{:S(2)}) async-start(), calls=%async_computation.21 | async-start | bytes 1966080 | tf_op jit(solution)/shard_map/reduce_scatter | solution.py:327
  834.2 246.6 %reduce-scatter.21.cloned.1.call-start = ((), (), s32[]{:S(2)}) async-start(), calls=%async_computation.20 | async-start | bytes 5898240 | tf_op jit(solution)/shard_map/reduce_scatter | solution.py:324
  838.0 267.1 %reduce-scatter.37.cloned.1.call-start = ((), (), s32[]{:S(2)}) async-start(), calls=%async_computation.28 | async-start | bytes 491520
  840.2 352.0 %reduce-scatter.39.cloned.1.call-start = ((), (), s32[]{:S(2)}) async-start(), calls=%async_computation.29 | async-start | bytes 5898240
  865.7 414.3 %reduce-scatter.29.cloned.1.call-start = ((), (), s32[]{:S(2)}) async-start(), calls=%async_computation.24 | async-start | bytes 5898240 | tf_op jit(solution)/shard_map/reduce_scatter | solution.py:345
  874.4 493.6 %reduce-scatter.27.cloned.1.call-start = ((), (), s32[]{:S(2)}) async-start(), calls=%async_computation.23 | async-start | bytes 5898240 | tf_op jit(solution)/shard_map/reduce_scatter | solution.py:342
  883.2 558.9 %all-reduce.7.cloned.1.call-start = ((), (), s32[]{:S(2)}) async-start(), calls=%async_computation.30 | async-start | bytes 6291456 | tf_op jit(solution)/shard_map/psum | solution.py:354
  1080.8 4.2 copy-start.3
  1080.8 4.8 copy-start.12
  1442.1 4.1 copy-start.19
  1442.1 5.8 copy-start.18
  (10 other events, 13.7 us)
Sparse Core Ops, SparseCore 0:
  9.6 39.7 all-gather.8
  50.9 35.8 all-gather.12
  89.3 22.2 all-gather.10
  113.0 89.4 all-gather.16
  204.8 21.8 all-gather.14
  228.2 89.3 all-gather.18
  758.5 32.6 reduce-scatter.32
  794.9 35.9 reduce-scatter.30
  833.2 85.2 reduce-scatter.34
  921.2 35.9 reduce-scatter.24
  960.1 34.2 reduce-scatter.22
  996.6 84.1 reduce-scatter.20
  1083.6 21.4 reduce-scatter.36
  1107.2 84.9 reduce-scatter.38
  1194.4 85.6 reduce-scatter.28
  1282.2 85.7 reduce-scatter.26
  1372.0 69.9 all-reduce.6
where the time goes:
time: 1470 us; the launch traced here: 1460 us
  waiting for transfers between devices  820 us (56%)
  blocking collectives  236 us (16%)
  matrix products  165 us (11%)
  local copies, waits for them, and re-layouts  147 us (10%)
  other arithmetic  60.9 us (4%)
  between operations  16.1 us (1%)
    unnamed x22, waiting for transfers between devices  106 us
    all_gather x1, waiting for transfers between devices, per_device(): lax.all_gather(w_query, 'fsdp', axis=0, tiled=True)  89.4 us
    reduce_scatter x1, waiting for transfers between devices, per_device(): lax.psum_scatter(grad_w_query.astype(jnp.bfloat16), 'fsdp', scatter_dimen...  86.3 us
    reduce_scatter x1, waiting for transfers between devices, per_device(): lax.psum_scatter(grad_w_gate.astype(jnp.bfloat16), 'fsdp', scatter_dimens...  85 us
    reduce_scatter x1, waiting for transfers between devices, per_device(): lax.psum_scatter(grad_w_up.astype(jnp.bfloat16), 'fsdp', scatter_dimensio...  82.4 us
    unnamed x133, local copies, waits for them, and re-layouts  71.1 us
    psum x1, waiting for transfers between devices, per_device(): lax.psum(reduced[1].astype(jnp.bfloat16), 'expert').astype(jnp.float32)  71 us
    all_gather x1, waiting for transfers between devices, per_device(): lax.all_gather(w_out, 'fsdp', axis=1, tiled=True)  68.2 us
  transfers between devices with their start and end apart: 19, of which 19 were waited for; matrix products, arithmetic and copies ran while one was open for 11% of the time, Pallas kernels for 0%

commit v1 on v0

v1 whole, which is shorter than its diff:
```python
import functools

import jax
import jax.numpy as jnp
from jax import lax
from jax.experimental import pallas as pl
from jax.experimental.pallas import tpu as pltpu
from jax.sharding import PartitionSpec as P

HEAD_DIM = 64
BLOCK = 256

EPSILON = 1e-06
RESIDUAL_SCALE = 0.22
ATTENTION_SCALE = 0.015625
ROPE_BASE = 10000.0
HIGHEST = lax.Precision.HIGHEST
MESH = pl.DeviceIdType.MESH
VMEM_LIMIT = 63_000_000
F32 = jnp.float32
BF16 = jnp.bfloat16
LANES = 128


def plane_neighbours():
    me = lax.axis_index("expert")
    core = lax.rem(me, 2)
    x_bit = lax.rem(me // 2, 2)
    y_bit = me // 4
    sibling = me + 1 - 2 * core
    x_peer = me + 2 - 4 * x_bit
    y_peer = me + 4 - 8 * y_bit
    diagonal = x_peer + 4 - 8 * y_bit
    return me, core, x_bit, y_bit, sibling, x_peer, y_peer, diagonal


def greet(axis, peers):
    barrier = pltpu.get_barrier_semaphore()
    for peer in peers:
        pl.semaphore_signal(barrier, inc=1, device_id={axis: peer}, device_id_type=MESH)
    pl.semaphore_wait(barrier, len(peers))


def gather_kernel(count, *refs):
    ins, outs = refs[:count], refs[count : 2 * count]
    own_sem, send_sem, recv_sem = refs[2 * count :]
    me, _, _, _, sibling, x_peer, y_peer, diagonal = plane_neighbours()
    greet("expert", (sibling, x_peer, y_peer))

    def remote(k, slot, source, target, peer):
        return pltpu.make_async_remote_copy(
            src_ref=source,
            dst_ref=target,
            send_sem=send_sem.at[k, slot],
            recv_sem=recv_sem.at[k, slot],
            device_id={"expert": peer},
            device_id_type=MESH,
        )

    plans = []
    for k in range(count):
        half = ins[k].shape[0] // 2
        parts = (pl.ds(0, half), pl.ds(half, half))
        out = outs[k]
        own = pltpu.make_async_copy(ins[k], out.at[me], own_sem.at[k])
        copies = [remote(k, 0, ins[k], out.at[me], sibling)]
        for h in range(2):
            copies.append(remote(k, 1 + h, ins[k].at[parts[h]], out.at[me, parts[h]], x_peer))
        for h in range(2):
            copies.append(remote(k, 3 + h, ins[k].at[parts[h]], out.at[me, parts[h]], y_peer))

        def forward(slot, block, h, peer):
            return remote(k, slot, out.at[block, parts[h]], out.at[block, parts[h]], peer)

        copies.append(forward(5, y_peer, 0, x_peer))
        copies.append(forward(6, x_peer, 1, y_peer))
        for h in range(2):
            copies.append(forward(7 + h, x_peer, h, sibling))
        for h in range(2):
            copies.append(forward(9 + h, y_peer, h, sibling))
        for h in range(2):
            copies.append(forward(11 + h, diagonal, h, sibling))
        plans.append((own, copies))
    for own, copies in plans:
        for slot in (3, 2, 1, 4, 0):
            copies[slot].start()
        own.start()
    for own, copies in plans:
        copies[3].wait_recv()
        copies[5].start()
        copies[2].wait_recv()
        copies[6].start()
        copies[9].start()
        copies[8].start()
        copies[1].wait_recv()
        copies[7].start()
        copies[4].wait_recv()
        copies[10].start()
    for own, copies in plans:
        copies[5].wait_recv()
        copies[11].start()
        copies[6].wait_recv()
        copies[12].start()
    for own, copies in plans:
        for slot in (0, 7, 8, 9, 10, 11, 12):
            copies[slot].wait_recv()
        for copy in copies:
            copy.wait_send()
        own.wait()


def plane_gather(arrays, collective_id):
    if lax.axis_size("expert") != 8:
        return [lax.all_gather(array, "expert", axis=0) for array in arrays]
    count = len(arrays)
    size = sum(array.size * array.dtype.itemsize for array in arrays)
    return pl.pallas_call(
        functools.partial(gather_kernel, count),
        out_shape=[jax.ShapeDtypeStruct((8,) + array.shape, array.dtype) for array in arrays],
        in_specs=[pl.BlockSpec(memory_space=pltpu.VMEM)] * count,
        out_specs=[pl.BlockSpec(memory_space=pl.ANY)] * count,
        scratch_shapes=[
            pltpu.SemaphoreType.DMA((count,)),
            pltpu.SemaphoreType.DMA((count, 13)),
            pltpu.SemaphoreType.DMA((count, 13)),
        ],
        compiler_params=pltpu.CompilerParams(
            collective_id=collective_id, has_side_effects=True, vmem_limit_bytes=VMEM_LIMIT
        ),
        cost_estimate=pl.CostEstimate(flops=0, bytes_accessed=16 * size, transcendentals=0),
        name="plane_gather",
    )(*arrays)


def scatter_kernel(count, *refs):
    ins, outs = refs[:count], refs[count : 2 * count]
    scratch = refs[2 * count : 2 * count + 6 * count]
    send_sem, recv_sem = refs[8 * count :]
    me, core, x_bit, y_bit, sibling, x_peer, y_peer, diagonal = plane_neighbours()
    greet("expert", (sibling, x_peer, y_peer))
    chip = me // 2
    chip_x, chip_y, chip_d = x_peer // 2, y_peer // 2, diagonal // 2
    order = (chip_d, chip_x, chip_y, chip)

    def remote(k, slot, source, target, peer):
        return pltpu.make_async_remote_copy(
            src_ref=source,
            dst_ref=target,
            send_sem=send_sem.at[k, slot],
            recv_sem=recv_sem.at[k, slot],
            device_id={"expert": peer},
            device_id_type=MESH,
        )

    stage0 = []
    for k in range(count):
        pair = scratch[6 * k]
        copies = [
            remote(k, i, ins[k].at[2 * order[i] + 1 - core], pair.at[i], sibling) for i in range(4)
        ]
        stage0.append(copies)
        for copy in copies:
            copy.start()
    later = []
    for k in range(count):
        pair, sums, first_x, first_y, second_x, second_y = scratch[6 * k : 6 * k + 6]
        rows = ins[k].shape[1]
        half = rows // 2
        parts = (pl.ds(0, half), pl.ds(half, half))
        dtype = ins[k].dtype

        def join(i):
            stage0[k][i].wait_recv()
            sums[i] = (ins[k][2 * order[i] + core].astype(F32) + pair[i].astype(F32)).astype(dtype)

        join(0)
        copies = [
            remote(k, 4, sums.at[0, parts[0]], first_x.at[1], x_peer),
            remote(k, 5, sums.at[0, parts[1]], first_y.at[1], y_peer),
        ]
        for copy in copies:
            copy.start()
        join(1)
        copies.append(remote(k, 6, sums.at[1, parts[0]], first_x.at[0], x_peer))
        copies[-1].start()
        join(2)
        copies.append(remote(k, 7, sums.at[2, parts[1]], first_y.at[0], y_peer))
        copies[-1].start()
        join(3)
        later.append(copies)
    for k in range(count):
        pair, sums, first_x, first_y, second_x, second_y = scratch[6 * k : 6 * k + 6]
        half = ins[k].shape[1] // 2
        parts = (pl.ds(0, half), pl.ds(half, half))
        dtype = ins[k].dtype
        copies = later[k]
        copies[0].wait_recv()
        pair[0, parts[0]] = (
            sums[2, parts[0]].astype(F32) + first_x[1].astype(F32)
        ).astype(dtype)
        copies.append(remote(k, 8, pair.at[0, parts[0]], second_y, y_peer))
        copies[-1].start()
        copies[1].wait_recv()
        pair[0, parts[1]] = (
            sums[1, parts[1]].astype(F32) + first_y[1].astype(F32)
        ).astype(dtype)
        copies.append(remote(k, 9, pair.at[0, parts[1]], second_x, x_peer))
        copies[-1].start()
    for k in range(count):
        pair, sums, first_x, first_y, second_x, second_y = scratch[6 * k : 6 * k + 6]
        half = ins[k].shape[1] // 2
        parts = (pl.ds(0, half), pl.ds(half, half))
        copies = later[k]
        copies[2].wait_recv()
        copies[4].wait_recv()
        outs[k][parts[0]] = (
            sums[3, parts[0]].astype(F32) + first_x[0].astype(F32) + second_y[...].astype(F32)
        )
        copies[3].wait_recv()
        copies[5].wait_recv()
        outs[k][parts[1]] = (
            sums[3, parts[1]].astype(F32) + first_y[0].astype(F32) + second_x[...].astype(F32)
        )
        for copy in stage0[k] + copies:
            copy.wait_send()


def plane_scatter(arrays, collective_id):
    if lax.axis_size("expert") != 8:
        return [
            lax.psum_scatter(array, "expert", scatter_dimension=0, tiled=False).astype(F32)
            for array in arrays
        ]
    count = len(arrays)
    scratch = []
    for array in arrays:
        _, rows, columns = array.shape
        half = rows // 2
        for shape in (
            (4, rows, columns),
            (4, rows, columns),
            (2, half, columns),
            (2, half, columns),
            (half, columns),
            (half, columns),
        ):
            scratch.append(pltpu.VMEM(shape, array.dtype))
    size = sum(array.size * array.dtype.itemsize for array in arrays)
    return pl.pallas_call(
        functools.partial(scatter_kernel, count),
        out_shape=[jax.ShapeDtypeStruct(array.shape[1:], F32) for array in arrays],
        in_specs=[pl.BlockSpec(memory_space=pltpu.VMEM)] * count,
        out_specs=[pl.BlockSpec(memory_space=pltpu.VMEM)] * count,
        scratch_shapes=scratch
        + [pltpu.SemaphoreType.DMA((count, 10)), pltpu.SemaphoreType.DMA((count, 10))],
        compiler_params=pltpu.CompilerParams(
            collective_id=collective_id, has_side_effects=True, vmem_limit_bytes=VMEM_LIMIT
        ),
        cost_estimate=pl.CostEstimate(flops=0, bytes_accessed=3 * size, transcendentals=0),
        name="plane_scatter",
    )(*arrays)


def line_greet(me, last):
    barrier = pltpu.get_barrier_semaphore()

    @pl.when(me > 0)
    def _():
        pl.semaphore_signal(barrier, inc=1, device_id={"fsdp": me - 1}, device_id_type=MESH)

    @pl.when(me < last)
    def _():
        pl.semaphore_signal(barrier, inc=1, device_id={"fsdp": me + 1}, device_id_type=MESH)

    @pl.when((me > 0) & (me < last))
    def _():
        pl.semaphore_wait(barrier, 2)

    @pl.when((me == 0) | (me == last))
    def _():
        pl.semaphore_wait(barrier, 1)


def line_gather_kernel(size, axes, *refs):
    count = len(axes)
    ins, outs = refs[:count], refs[count : 2 * count]
    own_sem, send_sem, recv_sem = refs[2 * count :]
    me = lax.axis_index("fsdp")
    last = size - 1
    line_greet(me, last)

    def place(k, owner):
        rows, columns = ins[k].shape
        if axes[k] == 0:
            return outs[k].at[pl.ds(pl.multiple_of(owner * rows, rows), rows)]
        return outs[k].at[:, pl.ds(pl.multiple_of(owner * columns, columns), columns)]

    def remote(k, side, step, owner, source=None):
        return pltpu.make_async_remote_copy(
            src_ref=place(k, owner) if source is None else source,
            dst_ref=place(k, owner),
            send_sem=send_sem.at[k, side, step],
            recv_sem=recv_sem.at[k, side, step],
            device_id={"fsdp": me + 1 - 2 * side},
            device_id_type=MESH,
        )

    own = [pltpu.make_async_copy(ins[k], place(k, me), own_sem.at[k]) for k in range(count)]
    for k in range(count):

        @pl.when(me < last)
        def _():
            remote(k, 0, 0, me, ins[k]).start()

        @pl.when(me > 0)
        def _():
            remote(k, 1, 0, me, ins[k]).start()

    for k in range(count):
        own[k].start()
    for step in range(size - 1):
        for k in range(count):
            @pl.when(me - 1 - step >= 0)
            def _():
                remote(k, 0, step, me - 1 - step).wait_recv()

                @pl.when(me < last)
                def _():
                    remote(k, 0, step + 1, me - 1 - step).start()

            @pl.when(me + 1 + step <= last)
            def _():
                remote(k, 1, step, me + 1 + step).wait_recv()

                @pl.when(me > 0)
                def _():
                    remote(k, 1, step + 1, me + 1 + step).start()

    for k in range(count):
        own[k].wait()
        for step in range(size - 1):

            @pl.when((me < last) & (me - step >= 0))
            def _():
                remote(k, 0, step, me - step).wait_send()

            @pl.when((me > 0) & (me + step <= last))
            def _():
                remote(k, 1, step, me + step).wait_send()


def line_gather(arrays, axes, collective_id):
    size = lax.axis_size("fsdp")
    if size != 4:
        return [
            lax.all_gather(array, "fsdp", axis=axis, tiled=True)
            for array, axis in zip(arrays, axes)
        ]
    count = len(arrays)
    shapes = []
    for array, axis in zip(arrays, axes):
        rows, columns = array.shape
        shapes.append((rows * size, columns) if axis == 0 else (rows, columns * size))
    return pl.pallas_call(
        functools.partial(line_gather_kernel, size, tuple(axes)),
        out_shape=[
            jax.ShapeDtypeStruct(shape, array.dtype) for shape, array in zip(shapes, arrays)
        ],
        in_specs=[pl.BlockSpec(memory_space=pltpu.VMEM)] * count,
        out_specs=[pl.BlockSpec(memory_space=pl.ANY)] * count,
        scratch_shapes=[
            pltpu.SemaphoreType.DMA((count,)),
            pltpu.SemaphoreType.DMA((count, 2, size)),
            pltpu.SemaphoreType.DMA((count, 2, size)),
        ],
        compiler_params=pltpu.CompilerParams(
            collective_id=collective_id, has_side_effects=True, vmem_limit_bytes=VMEM_LIMIT
        ),
        cost_estimate=pl.CostEstimate(flops=0, bytes_accessed=60_000_000, transcendentals=0),
        name="line_gather",
    )(*arrays)


def line_scatter_kernel(size, count, *refs):
    ins, outs = refs[: count + 1], refs[count + 1 : 2 * count + 2]
    scratch = refs[2 * count + 2 : 4 * count + 2]
    send_sem, recv_sem, note_send, note_recv, own_sem = refs[4 * count + 2 :]
    me = lax.axis_index("fsdp")
    last = size - 1
    line_greet(me, last)
    note_in, note_out = ins[count], outs[count]

    def remote(k, side, owner):
        sums, landed = scratch[2 * k], scratch[2 * k + 1]
        return pltpu.make_async_remote_copy(
            src_ref=sums.at[side, owner],
            dst_ref=landed.at[side, owner],
            send_sem=send_sem.at[k, side, owner],
            recv_sem=recv_sem.at[k, side, owner],
            device_id={"fsdp": me + 1 - 2 * side},
            device_id_type=MESH,
        )

    def note(side, hop, owner):
        return pltpu.make_async_remote_copy(
            src_ref=note_out.at[owner] if hop else note_in,
            dst_ref=note_out.at[owner],
            send_sem=note_send.at[side, hop],
            recv_sem=note_recv.at[side, hop],
            device_id={"fsdp": me + 1 - 2 * side},
            device_id_type=MESH,
        )

    own = pltpu.make_async_copy(note_in, note_out.at[me], own_sem)
    own.start()

    @pl.when(me < last)
    def _():
        note(0, 0, me).start()

    @pl.when(me > 0)
    def _():
        note(1, 0, me).start()

    def pass_on(k, side, owner, has_more):
        sums, landed = scratch[2 * k], scratch[2 * k + 1]

        @pl.when(has_more)
        def _():
            remote(k, side, owner).wait_recv()
            sums[side, owner] = (
                ins[k][owner].astype(F32) + landed[side, owner].astype(F32)
            ).astype(ins[k].dtype)

        @pl.when(jnp.logical_not(has_more))
        def _():
            sums[side, owner] = ins[k][owner]

        remote(k, side, owner).start()

    for far in range(size - 1):
        for k in range(count):
            right, left = last - far, far

            @pl.when(me < right)
            def _():
                pass_on(k, 0, right, me > 0)

            @pl.when(me > left)
            def _():
                pass_on(k, 1, left, me < last)

    for k in range(count):
        outs[k][...] = ins[k][me].astype(F32)
        for side, there in ((0, me > 0), (1, me < last)):

            @pl.when(there)
            def _():
                remote(k, side, me).wait_recv()
                outs[k][...] += scratch[2 * k + 1][side, me].astype(F32)

    for hop in range(size - 1):

        @pl.when(me - 1 - hop >= 0)
        def _():
            note(0, hop, me - 1 - hop).wait_recv()

            @pl.when(me < last)
            def _():
                note(0, hop + 1, me - 1 - hop).start()

        @pl.when(me + 1 + hop <= last)
        def _():
            note(1, hop, me + 1 + hop).wait_recv()

            @pl.when(me > 0)
            def _():
                note(1, hop + 1, me + 1 + hop).start()

    own.wait()
    for hop in range(size - 1):

        @pl.when((me < last) & (me - hop >= 0))
        def _():
            note(0, hop, me - hop).wait_send()

        @pl.when((me > 0) & (me + hop <= last))
        def _():
            note(1, hop, me + hop).wait_send()

    for k in range(count):
        for owner in range(size):

            @pl.when(me < owner)
            def _():
                remote(k, 0, owner).wait_send()

            @pl.when(me > owner)
            def _():
                remote(k, 1, owner).wait_send()


def line_scatter(arrays, notes, collective_id):
    size = lax.axis_size("fsdp")
    if size != 4:
        return [
            lax.psum_scatter(array, "fsdp", scatter_dimension=0, tiled=False).astype(F32)
            for array in arrays
        ] + [lax.all_gather(notes, "fsdp", axis=0)]
    count = len(arrays)
    scratch = []
    for array in arrays:
        scratch += [pltpu.VMEM((2,) + array.shape, array.dtype)] * 2
    return pl.pallas_call(
        functools.partial(line_scatter_kernel, size, count),
        out_shape=[jax.ShapeDtypeStruct(array.shape[1:], F32) for array in arrays]
        + [jax.ShapeDtypeStruct((size,) + notes.shape, notes.dtype)],
        in_specs=[pl.BlockSpec(memory_space=pltpu.VMEM)] * (count + 1),
        out_specs=[pl.BlockSpec(memory_space=pltpu.VMEM)] * (count + 1),
        scratch_shapes=scratch
        + [
            pltpu.SemaphoreType.DMA((count, 2, size)),
            pltpu.SemaphoreType.DMA((count, 2, size)),
            pltpu.SemaphoreType.DMA((2, size)),
            pltpu.SemaphoreType.DMA((2, size)),
            pltpu.SemaphoreType.DMA,
        ],
        compiler_params=pltpu.CompilerParams(
            collective_id=collective_id, has_side_effects=True, vmem_limit_bytes=VMEM_LIMIT
        ),
        cost_estimate=pl.CostEstimate(flops=0, bytes_accessed=60_000_000, transcendentals=0),
        name="line_scatter",
    )(*arrays, notes)


def dot(first, second, contract=(1, 0)):
    return lax.dot_general(
        first, second, (((contract[0],), (contract[1],)), ((), ())), preferred_element_type=F32
    )


def spin(values, cosine, sine):
    width = values.shape[1]
    half = HEAD_DIM // 2
    lane = lax.broadcasted_iota(jnp.int32, values.shape, 1)
    lower = lax.rem(lane, HEAD_DIM) < half
    swapped = jnp.where(
        lower, pltpu.roll(values, width - half, 1), pltpu.roll(values, half, 1)
    )
    return values * cosine + swapped * sine


def attend_kernel(
    per_group, x_ref, w_in_ref, w_out_ref, cos_ref, sin_ref,
    part_ref, a_ref, q_ref, k_ref, v_ref, o_ref, lse_ref,
):
    length, model_width = x_ref.shape
    query_width = per_group * HEAD_DIM
    turned = query_width + HEAD_DIM
    gain = w_out_ref[query_width : query_width + 1, :].astype(F32)

    def project(i, carry):
        rows = pl.ds(pl.multiple_of(i * BLOCK, BLOCK), BLOCK)
        x = x_ref[rows, :].astype(F32)
        inverse = lax.rsqrt(jnp.mean(x * x, axis=1, keepdims=True) + EPSILON)
        a = (x * inverse * gain).astype(BF16)
        a_ref[rows, :] = a
        pre = dot(a, w_in_ref[...])
        spun = spin(pre[:, :turned], cos_ref[rows, :], sin_ref[rows, :]).astype(BF16)
        for h in range(per_group):
            q_ref[h, rows, :] = spun[:, h * HEAD_DIM : (h + 1) * HEAD_DIM]
        k_ref[rows, :] = spun[:, query_width:turned]
        v_ref[rows, :] = pre[:, turned : turned + HEAD_DIM].astype(BF16)
        return carry

    lax.fori_loop(0, length // BLOCK, project, 0)
    for i in range(length // BLOCK):
        seen = (i + 1) * BLOCK
        rows = slice(i * BLOCK, seen)
        keys, values = k_ref[:seen, :], v_ref[:seen, :]
        for h in range(per_group):
            scores = dot(q_ref[h, rows, :], keys, (1, 1)) * ATTENTION_SCALE
            peak = jnp.max(scores, axis=1, keepdims=True)
            lifted = jnp.exp(scores - peak)
            total = jnp.sum(lifted, axis=1, keepdims=True)
            weights = (lifted * (1.0 / total)).astype(BF16)
            mixed = dot(weights, values)
            o_ref[rows, h * HEAD_DIM : (h + 1) * HEAD_DIM] = mixed.astype(BF16)
            lse_ref[h, rows, :] = peak + jnp.log(total)
        part_ref[rows, :] = dot(o_ref[rows, :], w_out_ref[:query_width, :]).astype(BF16)


def attend(x_all, w_in, w_out, cosine, sine, per_group):
    length, model_width = x_all.shape
    query_width = per_group * HEAD_DIM
    shapes = [
        jax.ShapeDtypeStruct((length, model_width), BF16),
        jax.ShapeDtypeStruct((length, model_width), BF16),
        jax.ShapeDtypeStruct((per_group, length, HEAD_DIM), BF16),
        jax.ShapeDtypeStruct((length, HEAD_DIM), BF16),
        jax.ShapeDtypeStruct((length, HEAD_DIM), BF16),
        jax.ShapeDtypeStruct((length, query_width), BF16),
        jax.ShapeDtypeStruct((per_group, length, 1), F32),
    ]
    return pl.pallas_call(
        functools.partial(attend_kernel, per_group),
        out_shape=shapes,
        in_specs=[pl.BlockSpec(memory_space=pltpu.VMEM)] * 5,
        out_specs=[pl.BlockSpec(memory_space=pltpu.VMEM)] * len(shapes),
        compiler_params=pltpu.CompilerParams(vmem_limit_bytes=VMEM_LIMIT),
        cost_estimate=pl.CostEstimate(
            flops=8_000_000_000, bytes_accessed=16_000_000, transcendentals=2_000_000
        ),
        name="attend",
    )(x_all, w_in, w_out, cosine, sine)


def attend_back_kernel(
    per_group, dw_ref, w_in_ref, w_out_ref, cos_ref, sin_ref,
    a_ref, q_ref, k_ref, v_ref, o_ref, lse_ref, b_ref, dl_ref,
    part_ref, gin_ref, gout_ref,
    turn_ref, dv_ref, back_ref,
):
    length, model_width = dw_ref.shape
    query_width = per_group * HEAD_DIM
    turned = query_width + HEAD_DIM
    blocks = length // BLOCK
    turn_ref[...] = jnp.zeros_like(turn_ref)
    dv_ref[...] = jnp.zeros_like(dv_ref)
    for i in range(blocks):
        seen = (i + 1) * BLOCK
        rows = slice(i * BLOCK, seen)
        keys, values = k_ref[:seen, :], v_ref[:seen, :]
        grad = dot(dw_ref[rows, :], w_out_ref[:query_width, :], (1, 1)).astype(BF16)
        for h in range(per_group):
            columns = slice(h * HEAD_DIM, (h + 1) * HEAD_DIM)
            queries = q_ref[h, rows, :]
            grad_head = grad[:, columns]
            scores = dot(queries, keys, (1, 1)) * ATTENTION_SCALE
            probs = jnp.exp(scores - lse_ref[h, rows, :])
            dv_ref[:seen, :] += dot(probs.astype(BF16), grad_head, (0, 0))
            grad_probs = dot(grad_head, values, (1, 1))
            inner = jnp.sum(probs * grad_probs, axis=1, keepdims=True)
            grad_scores = (probs * (grad_probs - inner)).astype(BF16)
            turn_ref[rows, columns] = dot(grad_scores, keys) * ATTENTION_SCALE
            turn_ref[:seen, query_width:turned] += (
                dot(grad_scores, queries, (0, 0)) * ATTENTION_SCALE
            )

    def unturn(i, carry):
        rows = pl.ds(pl.multiple_of(i * BLOCK, BLOCK), BLOCK)
        back_ref[rows, :turned] = spin(
            turn_ref[rows, :], cos_ref[rows, :], -sin_ref[rows, :]
        ).astype(BF16)
        back_ref[rows, turned : turned + HEAD_DIM] = dv_ref[rows, :].astype(BF16)
        part_ref[rows, :] = dot(
            back_ref[rows, : turned + HEAD_DIM], w_in_ref[:, : turned + HEAD_DIM], (1, 1)
        ).astype(BF16)
        return carry

    lax.fori_loop(0, blocks, unturn, 0)
    chunk = 384

    def weight_grads(i, carry):
        columns = pl.ds(pl.multiple_of(i * chunk, chunk), chunk)
        gin_ref[columns, : turned + HEAD_DIM] = dot(
            a_ref[:, columns], back_ref[:, : turned + HEAD_DIM], (0, 0)
        ).astype(BF16)
        gin_ref[columns, turned + HEAD_DIM :] = dot(
            b_ref[:, columns], dl_ref[...], (0, 0)
        )[:, : gin_ref.shape[1] - turned - HEAD_DIM].astype(BF16)
        gout_ref[:, columns] = dot(o_ref[...], dw_ref[:, columns], (0, 0)).astype(BF16)
        return carry

    lax.fori_loop(0, model_width // chunk, weight_grads, 0)


def attend_back(dw_all, w_in, w_out, cosine, sine, saved, b_all, dl_all, per_group):
    length, model_width = dw_all.shape
    query_width = per_group * HEAD_DIM
    turned = query_width + HEAD_DIM
    shapes = [
        jax.ShapeDtypeStruct((length, model_width), BF16),
        jax.ShapeDtypeStruct((model_width, w_in.shape[1]), BF16),
        jax.ShapeDtypeStruct((query_width, model_width), BF16),
    ]
    return pl.pallas_call(
        functools.partial(attend_back_kernel, per_group),
        out_shape=shapes,
        in_specs=[pl.BlockSpec(memory_space=pltpu.VMEM)] * 13,
        out_specs=[pl.BlockSpec(memory_space=pltpu.VMEM)] * len(shapes),
        scratch_shapes=[
            pltpu.VMEM((length, turned), F32),
            pltpu.VMEM((length, HEAD_DIM), F32),
            pltpu.VMEM((length, w_in.shape[1]), BF16),
        ],
        compiler_params=pltpu.CompilerParams(vmem_limit_bytes=VMEM_LIMIT),
        cost_estimate=pl.CostEstimate(
            flops=20_000_000_000, bytes_accessed=30_000_000, transcendentals=2_000_000
        ),
        name="attend_back",
    )(dw_all, w_in, w_out, cosine, sine, *saved, b_all, dl_all)


def experts_kernel(
    here, capacity, parts, lane_parts,
    me_ref, b_ref, dy_ref, g_ref, gate_ref, up_ref, down_ref,
    out_ref, db_ref, dg_ref, dgate_ref, dup_ref, ddown_ref,
    pick_ref, x_ref, y_ref, scale_ref, hidden_ref, dgp_ref, dup_s_ref, de_ref, inner_ref,
):
    step = pl.program_id(0)
    sources, tokens, model_width = b_ref.shape
    rows_all = sources * capacity
    slots = here * capacity
    first = me_ref[0, 0] * here

    @pl.when(step == 0)
    def _():
        row = lax.broadcasted_iota(jnp.int32, (tokens, tokens), 0)
        column = lax.broadcasted_iota(jnp.int32, (tokens, tokens), 1)
        earlier = (column < row).astype(BF16)
        lane = lax.broadcasted_iota(jnp.int32, (tokens, g_ref.shape[2]), 1)
        slot = lax.broadcasted_iota(jnp.int32, (tokens, slots), 1)

        def collect(j, carry):
            gates = g_ref[j]
            named = (gates >= 0.0).astype(BF16)
            rank = dot(earlier, named)
            picks = jnp.zeros((tokens, slots), F32)
            scaled = jnp.zeros((tokens, slots), F32)
            for e in range(here):
                mine = lane == first + e
                place = jnp.sum(jnp.where(mine, rank, 0.0), axis=1, keepdims=True)
                gate = jnp.sum(jnp.where(mine, gates, 0.0), axis=1, keepdims=True)
                hit = (slot - e * capacity == place.astype(jnp.int32)) & (gate >= 0.0)
                hit = hit & (slot >= e * capacity) & (slot < (e + 1) * capacity)
                picks = jnp.where(hit, 1.0, picks)
                scaled = jnp.where(hit, gate, scaled)
            pick = picks.astype(BF16)
            pick_ref[j] = pick
            ones = jnp.ones((tokens, LANES), F32)
            scales = lax.dot_general(
                scaled, ones, (((0,), (0,)), ((), ())), precision=HIGHEST,
                preferred_element_type=F32,
            )
            x = dot(pick, b_ref[j], (0, 0)).astype(BF16)
            y = dot(pick, dy_ref[j], (0, 0)).astype(BF16)
            at = pl.ds(pl.multiple_of(j * capacity, capacity), capacity)
            for e in range(here):
                piece = slice(e * capacity, (e + 1) * capacity)
                x_ref[e, at, :] = x[piece]
                y_ref[e, at, :] = y[piece]
                scale_ref[e, at, :] = scales[piece]
            return carry

        lax.fori_loop(0, sources, collect, 0)

    tile = min(256, rows_all)

    def rows_of(i, carry):
        rows = pl.ds(pl.multiple_of(i * tile, tile), tile)
        x = x_ref[step, rows, :]
        gate_pre = dot(x, gate_ref[0])
        up_pre = dot(x, up_ref[0])
        sigmoid = 1.0 / (1.0 + jnp.exp(-gate_pre))
        silu = gate_pre * sigmoid
        hidden = (silu * up_pre).astype(BF16)
        hidden_ref[rows, :] = hidden
        produced = dot(hidden, down_ref[0])
        scale = scale_ref[step, rows, 0:1]
        dy = RESIDUAL_SCALE * y_ref[step, rows, :].astype(F32)
        inner_ref[step, rows, :] = jnp.broadcast_to(
            jnp.sum(dy * produced, axis=1, keepdims=True), (tile, LANES)
        )
        grad = (scale * dy).astype(BF16)
        de_ref[rows, :] = grad
        y_ref[step, rows, :] = (scale * produced).astype(BF16)
        grad_hidden = dot(grad, down_ref[0], (1, 1))
        grad_gate = (
            grad_hidden * up_pre * sigmoid * (1.0 + gate_pre * (1.0 - sigmoid))
        ).astype(BF16)
        grad_up = (grad_hidden * silu).astype(BF16)
        dgp_ref[rows, :] = grad_gate
        dup_s_ref[rows, :] = grad_up
        return carry

    lax.fori_loop(0, rows_all // tile, rows_of, 0)
    width = model_width // parts

    def weight_grads(p, carry):
        columns = pl.ds(pl.multiple_of(p * width, width), width)
        x = x_ref[step, :, columns]
        dgate_ref[p, 0] = dot(x, dgp_ref[...], (0, 0)).astype(BF16)
        dup_ref[p, 0] = dot(x, dup_s_ref[...], (0, 0)).astype(BF16)
        return carry

    def down_grads(p, carry):
        columns = pl.ds(pl.multiple_of(p * width, width), width)
        ddown_ref[p, 0] = dot(hidden_ref[...], de_ref[:, columns], (0, 0)).astype(BF16)
        return carry

    if lane_parts:
        lax.fori_loop(0, parts, weight_grads, 0)
        lax.fori_loop(0, parts, down_grads, 0)
    else:
        for p in range(parts):
            columns = slice(p * width, (p + 1) * width)
            x = x_ref[step, :, columns]
            dgate_ref[p, 0] = dot(x, dgp_ref[...], (0, 0)).astype(BF16)
            dup_ref[p, 0] = dot(x, dup_s_ref[...], (0, 0)).astype(BF16)
        ddown_ref[0, 0] = dot(hidden_ref[...], de_ref[...], (0, 0)).astype(BF16)

    def rows_back(i, carry):
        rows = pl.ds(pl.multiple_of(i * tile, tile), tile)
        x_ref[step, rows, :] = (
            dot(dgp_ref[rows, :], gate_ref[0], (1, 1)) + dot(dup_s_ref[rows, :], up_ref[0], (1, 1))
        ).astype(BF16)
        return carry

    lax.fori_loop(0, rows_all // tile, rows_back, 0)

    @pl.when(step == here - 1)
    def _():
        lane = lax.broadcasted_iota(jnp.int32, (tokens, dg_ref.shape[2]), 1)

        def spread(j, carry):
            at = pl.ds(pl.multiple_of(j * capacity, capacity), capacity)
            pick = pick_ref[j]
            made = jnp.concatenate([y_ref[e, at, :] for e in range(here)], axis=0)
            out_ref[j] = dot(pick, made).astype(BF16)
            back = jnp.concatenate([x_ref[e, at, :] for e in range(here)], axis=0)
            db_ref[j] = dot(pick, back).astype(BF16)
            inner = jnp.concatenate([inner_ref[e, at, :] for e in range(here)], axis=0)
            place = lax.broadcasted_iota(jnp.int32, inner.shape, 0)
            target = lax.broadcasted_iota(jnp.int32, inner.shape, 1)
            owner = jnp.zeros(inner.shape, jnp.int32) + first
            for e in range(1, here):
                owner = jnp.where(place >= e * capacity, first + e, owner)
            inner = jnp.where(target == owner, inner, 0.0)
            dg_ref[j] = lax.dot_general(
                pick.astype(F32), inner, (((1,), (0,)), ((), ())), precision=HIGHEST,
                preferred_element_type=F32,
            )
            return carry

        lax.fori_loop(0, sources, spread, 0)


def experts(me, b_all, dy_all, g_all, w_gate, w_up, w_down, capacity, parts):
    sources, tokens, model_width = b_all.shape
    here, _, hidden_width = w_gate.shape
    rows_all = sources * capacity
    slots = here * capacity
    width = model_width // parts
    lane_parts = width % LANES == 0
    whole = lambda shape: pl.BlockSpec(
        shape, lambda e: (0,) * len(shape), pipeline_mode=pl.Buffered(1)
    )
    if lane_parts:
        down_shape = (parts, here, hidden_width, width)
    else:
        down_shape = (1, here, hidden_width, model_width)
    weight_shape = (parts, here, width, hidden_width)
    return pl.pallas_call(
        functools.partial(experts_kernel, here, capacity, parts, lane_parts),
        out_shape=[
            jax.ShapeDtypeStruct(b_all.shape, BF16),
            jax.ShapeDtypeStruct(b_all.shape, BF16),
            jax.ShapeDtypeStruct((sources, tokens, LANES), F32),
            jax.ShapeDtypeStruct(weight_shape, BF16),
            jax.ShapeDtypeStruct(weight_shape, BF16),
            jax.ShapeDtypeStruct(down_shape, BF16),
        ],
        grid=(here,),
        in_specs=[
            pl.BlockSpec(memory_space=pltpu.SMEM),
            whole(b_all.shape),
            whole(b_all.shape),
            whole(g_all.shape),
            pl.BlockSpec((1, model_width, hidden_width), lambda e: (e, 0, 0)),
            pl.BlockSpec((1, model_width, hidden_width), lambda e: (e, 0, 0)),
            pl.BlockSpec((1, hidden_width, model_width), lambda e: (e, 0, 0)),
        ],
        out_specs=[
            whole(b_all.shape),
            whole(b_all.shape),
            whole((sources, tokens, LANES)),
            pl.BlockSpec((parts, 1, width, hidden_width), lambda e: (0, e, 0, 0)),
            pl.BlockSpec((parts, 1, width, hidden_width), lambda e: (0, e, 0, 0)),
            pl.BlockSpec((down_shape[0], 1) + down_shape[2:], lambda e: (0, e, 0, 0)),
        ],
        scratch_shapes=[
            pltpu.VMEM((sources, tokens, slots), BF16),
            pltpu.VMEM((here, rows_all, model_width), BF16),
            pltpu.VMEM((here, rows_all, model_width), BF16),
            pltpu.VMEM((here, rows_all, LANES), F32),
            pltpu.VMEM((rows_all, hidden_width), BF16),
            pltpu.VMEM((rows_all, hidden_width), BF16),
            pltpu.VMEM((rows_all, hidden_width), BF16),
            pltpu.VMEM((rows_all, model_width), BF16),
            pltpu.VMEM((here, rows_all, LANES), F32),
        ],
        compiler_params=pltpu.CompilerParams(
            dimension_semantics=("arbitrary",), vmem_limit_bytes=VMEM_LIMIT
        ),
        cost_estimate=pl.CostEstimate(
            flops=26_000_000_000, bytes_accessed=42_000_000, transcendentals=1_000_000
        ),
        name="experts",
    )(me, b_all, dy_all, g_all, w_gate, w_up, w_down)


def norm_back(grad_normed, normed, inverse):
    return inverse * (grad_normed - normed * jnp.mean(grad_normed * normed, axis=-1, keepdims=True))


def rotary_tables(length, heads):
    half = HEAD_DIM // 2
    exponent = jnp.arange(half, dtype=F32) * (2.0 / HEAD_DIM)
    angles = jnp.arange(length, dtype=F32)[:, None] * jnp.power(ROPE_BASE, -exponent)[None, :]
    cosine, sine = jnp.cos(angles), jnp.sin(angles)
    cosine = jnp.concatenate([cosine, cosine] * heads, axis=1)
    sine = jnp.concatenate([-sine, sine] * heads, axis=1)
    return cosine, sine


def per_device(
    residual_in, cotangent, gain_attn, w_query, w_key, w_value, w_out, gain_ffn, w_router,
    w_gate, w_up, w_down, route_ids,
):
    me = lax.axis_index("expert")
    peers = lax.axis_size("expert")
    lines = lax.axis_size("fsdp")
    tokens, model_width = residual_in.shape[1:]
    length = tokens * peers
    groups = w_key.shape[1] // HEAD_DIM
    per_group = w_query.shape[1] // w_key.shape[1]
    query_width = per_group * HEAD_DIM
    experts_all = w_router.shape[1]
    here = w_gate.shape[0]
    top_count = route_ids.shape[2]
    capacity = (3 * tokens * top_count // (2 * experts_all) + 7) // 8 * 8
    shard = w_query.shape[0]
    turned = query_width + HEAD_DIM
    in_width = -(-(turned + HEAD_DIM + experts_all) // LANES) * LANES

    w_in_shard = jnp.concatenate(
        [
            lax.dynamic_slice(w_query, (0, me * query_width), (shard, query_width)),
            lax.dynamic_slice(w_key, (0, me * HEAD_DIM), (shard, HEAD_DIM)),
            lax.dynamic_slice(w_value, (0, me * HEAD_DIM), (shard, HEAD_DIM)),
            w_router,
            jnp.zeros((shard, in_width - turned - HEAD_DIM - experts_all), BF16),
        ],
        axis=1,
    )
    w_out_shard = jnp.concatenate(
        [
            lax.dynamic_slice(w_out, (me * query_width, 0), (query_width, shard)),
            gain_attn[None],
            gain_ffn[None],
            jnp.zeros((14, shard), BF16),
        ],
        axis=0,
    )
    x_all, dy_all = plane_gather([residual_in[0], cotangent[0]], 0)
    w_in, w_out_rows = line_gather([w_in_shard, w_out_shard], (0, 1), 1)
    gain_one = w_out_rows[query_width][None].astype(F32)
    gain_two = w_out_rows[query_width + 1][None].astype(F32)
    router = w_in[:, turned + HEAD_DIM : turned + HEAD_DIM + experts_all]
    cosine, sine = rotary_tables(length, per_group + 1)

    part, *saved = attend(
        x_all.reshape(length, model_width), w_in, w_out_rows, cosine, sine, per_group
    )
    (branch,) = plane_scatter([part.reshape(peers, tokens, model_width)], 2)

    rows = residual_in[0].astype(F32)
    inverse_one = lax.rsqrt(jnp.mean(rows * rows, axis=-1, keepdims=True) + EPSILON)
    normed_one = rows * inverse_one
    middle = rows + RESIDUAL_SCALE * branch
    inverse_two = lax.rsqrt(jnp.mean(middle * middle, axis=-1, keepdims=True) + EPSILON)
    normed_two = middle * inverse_two
    routed = (normed_two * gain_two).astype(BF16)
    logits = jnp.dot(routed, router, preferred_element_type=F32)
    chosen = jnp.any(
        route_ids[0][:, :, None] == jnp.arange(experts_all, dtype=jnp.int32)[None, None, :], axis=1
    )
    kept = jnp.where(chosen, logits, -jnp.inf)
    lifted = jnp.exp(kept - jnp.max(kept, axis=-1, keepdims=True))
    gates = lifted / jnp.sum(lifted, axis=-1, keepdims=True)
    marked = jnp.pad(
        jnp.where(chosen, gates, -1.0),
        ((0, 0), (0, LANES - experts_all)),
        constant_values=-1.0,
    )
    b_all, g_all = plane_gather([routed, marked], 3)

    sum_part, db_part, dg_part, dgate, dup, ddown = experts(
        me.reshape(1, 1), b_all, dy_all, g_all, w_gate, w_up, w_down, capacity, lines
    )
    if ddown.shape[0] != lines:
        ddown = ddown[0].reshape(here, -1, lines, shard).transpose(2, 0, 1, 3)
    db_sum, dg_sum = plane_scatter([db_part, dg_part], 4)

    grad_rows = cotangent[0].astype(F32)
    dg = dg_sum[:, :experts_all]
    grad_chosen = gates * (dg - jnp.sum(gates * dg, axis=-1, keepdims=True))
    grad_logits = grad_chosen.astype(BF16)
    grad_routed = (
        lax.dot_general(
            grad_logits, router, (((1,), (1,)), ((), ())), preferred_element_type=F32
        )
        + db_sum
    )
    grad_gain_two = jnp.sum(grad_routed * normed_two, axis=0)
    grad_middle = grad_rows + norm_back(grad_routed * gain_two, normed_two, inverse_two)
    grad_branch = (RESIDUAL_SCALE * grad_middle).astype(BF16)
    dw_all, dl_all = plane_gather(
        [grad_branch, jnp.pad(grad_logits, ((0, 0), (0, LANES - experts_all)))], 5
    )

    da_part, grad_in, grad_out = attend_back(
        dw_all.reshape(length, model_width), w_in, w_out_rows, cosine, sine, saved,
        b_all.reshape(length, model_width), dl_all.reshape(length, LANES), per_group,
    )
    da_sum, expert_sum = plane_scatter(
        [da_part.reshape(peers, tokens, model_width), sum_part], 6
    )

    outcome = middle + RESIDUAL_SCALE * expert_sum
    grad_gain_one = jnp.sum(da_sum * normed_one, axis=0)
    grad_input = grad_middle + norm_back(da_sum * gain_one, normed_one, inverse_one)
    squares = jnp.stack(
        [jnp.sum(v * v) for v in (rows, middle, outcome, grad_middle, grad_input)]
    )
    notes = jnp.broadcast_to(jnp.pad(squares, (0, 3))[:, None], (8, LANES))

    grad_out = jnp.concatenate(
        [
            grad_out,
            grad_gain_one.astype(BF16)[None],
            grad_gain_two.astype(BF16)[None],
            jnp.zeros((14, model_width), BF16),
        ],
        axis=0,
    )
    in_sum, out_sum, line_notes = line_scatter(
        [
            grad_in.reshape(lines, shard, in_width),
            grad_out.reshape(-1, lines, shard).transpose(1, 0, 2),
        ],
        notes,
        7,
    )
    in_all, out_all, notes_all = plane_gather(
        [in_sum.astype(BF16), out_sum.astype(BF16), jnp.sum(line_notes, axis=0)], 8
    )

    def columns_of(start, stop):
        return in_all[:, :, start:stop].transpose(1, 0, 2).reshape(shard, -1).astype(F32)

    count = tokens * model_width * lines * peers
    root_means = jnp.sqrt(jnp.sum(notes_all, axis=0)[:5, 0] / count)
    reduced = [
        lax.psum_scatter(array, "fsdp", scatter_dimension=0, tiled=False).astype(F32)
        for array in (dgate, dup, ddown)
    ]
    gain_rows = jnp.sum(out_all[:, query_width : query_width + 2, :].astype(F32), axis=0)
    return (
        outcome.astype(BF16)[None],
        grad_input.astype(BF16)[None],
        gain_rows[0],
        columns_of(0, query_width),
        columns_of(query_width, turned),
        columns_of(turned, turned + HEAD_DIM),
        out_all[:, :query_width, :].reshape(groups * query_width, shard).astype(F32),
        gain_rows[1],
        in_all[0, :, turned + HEAD_DIM : turned + HEAD_DIM + experts_all].astype(F32),
        reduced[0],
        reduced[1],
        reduced[2],
        root_means,
    )


def solution(mesh):
    in_specs = (
        P("fsdp", "expert", None),
        P("fsdp", "expert", None),
        P("fsdp"),
        P("fsdp", None),
        P("fsdp", None),
        P("fsdp", None),
        P(None, "fsdp"),
        P("fsdp"),
        P("fsdp", None),
        P("expert", None, None),
        P("expert", None, None),
        P("expert", None, None),
        P("fsdp", "expert", None),
    )
    out_specs = (
        P("fsdp", "expert", None),
        P("fsdp", "expert", None),
        P("fsdp"),
        P("fsdp", None),
        P("fsdp", None),
        P("fsdp", None),
        P(None, "fsdp"),
        P("fsdp"),
        P("fsdp", None),
        P("expert", "fsdp", None),
        P("expert", "fsdp", None),
        P("expert", None, "fsdp"),
        P(),
    )
    return jax.shard_map(
        per_device, mesh=mesh, in_specs=in_specs, out_specs=out_specs, check_vma=False
    )
```

time: 1470 us -> 516 us (0.35)
  waiting for transfers between devices: 820 us -> 28.8 us
  Pallas kernels: 0 us -> 387 us
  blocking collectives: 236 us -> 0 us
  matrix products: 165 us -> 3.34 us
  local copies, waits for them, and re-layouts: 147 us -> 34.8 us
  other arithmetic: 60.9 us -> 38.5 us
    pallas_call x0 -> x12, Pallas kernels: none -> 387 us  [the longest x4 93.4 us: plane_gather(): pl.pallas_call(functools.partial(gather_kernel, count), out_shape=[jax.Sh...]
    reduce_scatter x5 -> x3, waiting for transfers between devices: 327 us -> 27.4 us  [per_device(): lax.psum_scatter(array, 'fsdp', scatter_dimension=0, tiled=False)]
    all_gather x6 -> x0, waiting for transfers between devices: 231 us -> none  [the longest x1 89.4 us: per_device(): lax.all_gather(w_query, 'fsdp', axis=0, tiled=True)]
    dot_general x82 -> x2, matrix products: 165 us -> 3.34 us  [the longest x1 1.77 us: per_device(): lax.dot_general(grad_logits, router, (((1,), (1,)), ((), ())), preferred_...]
    all_to_all x2 -> x0, blocking collectives: 118 us -> none  [the longest x1 59 us: per_device(): lax.all_to_all(outgoing.reshape(peer_count, experts_here, capacity, model...]
    unnamed x22 -> x3, waiting for transfers between devices: 106 us -> 1.39 us
    all_to_all x2 -> x0, waiting for transfers between devices: 84.5 us -> none  [the longest x1 45.4 us: per_device(): lax.all_to_all(grad_received, 'expert', split_axis=0, concat_axis=0, tile...]
    psum x1 -> x0, waiting for transfers between devices: 71 us -> none  [per_device(): lax.psum(reduced[1].astype(jnp.bfloat16), 'expert').astype(jnp.float32)]
  transfers between devices with their start and end apart: 19 -> 3, of which waited for: 19 -> 1; matrix products, arithmetic and copies ran while one was open for 11% -> 10% of each run, Pallas kernels for 0% -> 42%
where the time goes in v1:
time: 516 us; the launch traced here: 507 us
  Pallas kernels  387 us (75%)
  other arithmetic  38.5 us (7%)
  local copies, waits for them, and re-layouts  34.8 us (7%)
  waiting for transfers between devices  28.8 us (6%)
  between operations  14.5 us (3%)
    pallas_call x4, Pallas kernels, plane_gather(): pl.pallas_call(functools.partial(gather_kernel, count), out_shape=[jax.Sh...  93.4 us
    pallas_call x1, Pallas kernels, line_scatter(): pl.pallas_call(functools.partial(line_scatter_kernel, size, count), out_s...  87.5 us
    pallas_call x3, Pallas kernels, plane_scatter(): pl.pallas_call(functools.partial(scatter_kernel, count), out_shape=[jax.S...  77.7 us
    pallas_call x1, Pallas kernels, experts(): pl.pallas_call(functools.partial(experts_kernel, here, capacity, parts, l...  51.6 us
    pallas_call x1, Pallas kernels, line_gather(): pl.pallas_call(functools.partial(line_gather_kernel, size, tuple(axes)),...  35.7 us
    reduce_scatter x3, waiting for transfers between devices, per_device(): lax.psum_scatter(array, 'fsdp', scatter_dimension=0, tiled=False)  27.4 us
    pallas_call x1, Pallas kernels, attend_back(): pl.pallas_call(functools.partial(attend_back_kernel, per_group), out_shap...  24.5 us
    pallas_call x1, Pallas kernels, attend(): pl.pallas_call(functools.partial(attend_kernel, per_group), out_shape=sha...  16.2 us
  transfers between devices with their start and end apart: 3, of which 1 were waited for; matrix products, arithmetic and copies ran while one was open for 10% of the time, Pallas kernels for 42%

profile of v1, /device:TPU:0, one launch (start us, length us, event | category | flops | bytes accessed | tf_op | source)
XLA Modules:
  0.0 506.6 jit_solution(12762640578348464306)
XLA Ops:
  7.3 0.8 broadcast_in_dim.24
  8.0 0.7 broadcast_in_dim.48
  8.7 0.7 fusion.15
  9.5 0.8 copy.69
  10.4 1.1 constant_dynamic-slice_fusion.3
  11.6 1.1 constant_dynamic-slice_fusion.1
  12.7 0.8 maximum_maximum_fusion.refs_1_
  13.5 0.9 concatenate.18.refs_0_
  14.4 35.7 %line_gather.1 = (bf16[1536,384]{1,0:T(8,128)(2,1)}, bf16[208,1536]{1,0:T(8,128)(2,1)}) custom-call(bf16[384,384]{1,0:T(8,128)(2,1)} %concatenate.18.refs_0_, bf16[208,384]{1,0:T(8,128)(2,1)} %maximum_maximum_fusion.refs_1_), custom_call_target="tpu_custom_call" | custom-call | bytes 60000000 | tf_op jit(solution)/shard_map/line_gather/pallas_call | solution.py:364
  50.1 0.9 convert_reduce_fusion.1
  50.9 2.0 fusion.10
  52.9 4.3 concatenate.20.cos_ref
  57.2 4.1 concatenate.21.sin_ref
  61.4 31.5 %plane_gather.4 = (bf16[8,128,1536]{2,1,0:T(8,128)(2,1)}, bf16[8,128,1536]{2,1,0:T(8,128)(2,1)}) custom-call(bf16[128,1536]{1,0:T(8,128)(2,1)} %bitcast.64, bf16[128,1536]{1,0:T(8,128)(2,1)} %bitcast.70), custom_call_target="tpu_custom_call" | custom-call | bytes 12582912 | tf_op jit(solution)/shard_map/plane_gather/pallas_call | solution.py:117
  92.9 16.2 %attend.1 = (bf16[1024,1536]{1,0:T(8,128)(2,1)}, bf16[1024,1536]{1,0:T(8,128)(2,1)}, bf16[3,1024,64]{2,1,0:T(8,128)(2,1)}, bf16[1024,64]{1,0:T(8,128)(2,1)}, bf1...) custom-call(bf16[1024,1536]{1,0:T(8,128)(2,1)} %bitcast.77, ...), custom_call_target="tpu_custom_call" | custom-call | flops 8000000000 | bytes 16000000 | tf_op jit(solution)/shard_map/attend/pallas_call | solution.py:605
  109.1 20.5 %plane_scatter.3 = f32[128,1536]{1,0:T(8,128)} custom-call(bf16[8,128,1536]{2,1,0:T(8,128)(2,1)} %bitcast.68), custom_call_target="tpu_custom_call" | custom-call | bytes 9437184 | tf_op jit(solution)/shard_map/plane_scatter/pallas_call | solution.py:249
  129.6 2.1 fusion.3
  131.8 1.6 fusion.19
  133.7 0.6 pad.12.refs_1_
  134.4 20.6 %plane_gather.5 = (bf16[8,128,1536]{2,1,0:T(8,128)(2,1)}, f32[8,128,128]{2,1,0:T(8,128)}) custom-call(bf16[128,1536]{1,0:T(8,128)(2,1)} %copy-done.5, f32[128,128]{1,0:T(8,128)} %pad.12.refs_1_), custom_call_target="tpu_custom_call" | custom-call | bytes 7340032 | tf_op jit(solution)/shard_map/plane_gather/pallas_call | solution.py:117
  155.0 51.6 %experts.1 = (bf16[8,128,1536]{2,1,0:T(8,128)(2,1)}, bf16[8,128,1536]{2,1,0:T(8,128)(2,1)}, f32[8,128,128]{2,1,0:T(8,128)}, bf16[4,3,384,512]{3,2,1,0:T(8,128)(2...) custom-call(s32[1,1]{1,0:T(1,128)} %bitcast.5.me_ref, ...), custom_call_target="tpu_custom_call" | custom-call | flops 25999998976 | bytes 42000000 | tf_op jit(solution)/shard_map/experts/pallas_call | solution.py:864
  206.7 0.7 reduce-scatter.6.cloned.1.call-update
  207.4 0.7 reduce-scatter.4.cloned.1.call-update
  208.1 22.7 %plane_scatter.4 = (f32[128,1536]{1,0:T(8,128)}, f32[128,128]{1,0:T(8,128)}) custom-call(bf16[8,128,1536]{2,1,0:T(8,128)(2,1)} %get-tuple-element.54.refs_0_, f32[8,128,128]{2,1,0:T(8,128)} %get-tuple-element.55.refs_1_), custom_call_target="tpu_custom_call" | custom-call | bytes 11010048 | tf_op jit(solution)/shard_map/plane_scatter/pallas_call | solution.py:249
  230.9 1.1 multiply_reduce_fusion.7
  231.9 1.0 multiply_convert_fusion.2
  232.9 0.6 pad.13.refs_1_
  233.5 1.8 multiply_reduce_fusion.3
  235.3 1.0 multiply_reduce_fusion.1
  236.4 0.8 multiply_convert_fusion.refs_0_
  237.2 19.4 %plane_gather.6 = (bf16[8,128,1536]{2,1,0:T(8,128)(2,1)}, bf16[8,128,128]{2,1,0:T(8,128)(2,1)}) custom-call(bf16[128,1536]{1,0:T(8,128)(2,1)} %multiply_convert_fusion.refs_0_, bf16[128,128]{1,0:T(8,128)(2,1)} %pad.13.refs_1_), custom_call_target="tpu_custom_call" | custom-call | bytes 6815744 | tf_op jit(solution)/shard_map/plane_gather/pallas_call | solution.py:117
  256.6 24.5 %attend_back.1 = (bf16[1024,1536]{1,0:T(8,128)(2,1)}, bf16[1536,384]{1,0:T(8,128)(2,1)}, bf16[192,1536]{1,0:T(8,128)(2,1)}) custom-call(bf16[1024,1536]{1,0:T(8,128)(2,1)} %bitcast.76, bf16[1536,384]{1,0:T(8,128)(2,1)} %get-tuple-element.48.w_in_ref, bf16[208,1536]{1,0:T(8,128)(2,1)} %get-tuple-element.49.w_out_ref, f32[1024,256]{1,0:T(8,128)} %concatenate.20.cos_ref, ...), custom_call_target="tpu_custom_call" | custom-call | flops 20000000000 | bytes 30000000 | tf_op jit(solution)/shard_map/attend_back/pallas_call | solution.py:687
  281.1 34.5 %plane_scatter.5 = (f32[128,1536]{1,0:T(8,128)}, f32[128,1536]{1,0:T(8,128)}) custom-call(bf16[8,128,1536]{2,1,0:T(8,128)(2,1)} %bitcast.65, bf16[8,128,1536]{2,1,0:T(8,128)(2,1)} %get-tuple-element.67.refs_1_), custom_call_target="tpu_custom_call" | custom-call | bytes 18874368 | tf_op jit(solution)/shard_map/plane_scatter/pallas_call | solution.py:249
  315.6 1.5 fusion.9
  317.2 1.2 copy.86
  318.4 1.5 multiply_reduce_fusion.2
  319.9 1.6 multiply_reduce_fusion
  321.5 3.3 stack.23
  324.8 1.0 maximum_bitcast_fusion.refs_1_
  325.9 0.7 broadcast_in_dim.55.refs_2_
  326.5 87.5 %line_scatter.1 = (f32[384,384]{1,0:T(8,128)}, f32[208,384]{1,0:T(8,128)}, f32[4,8,128]{2,1,0:T(8,128)}) custom-call(bf16[4,384,384]{2,1,0:T(8,128)(2,1)} %bitcast.71, bf16[4,208,384]{2,1,0:T(8,128)(2,1)} %maximum_bitcast_fusion.refs_1_, f32[8,128]{1,0:T(8,128)} %broadcast_in_dim.55.refs_2_), custom_call_target="tpu_custom_call" | custom-call | bytes 60000000 | tf_op jit(solution)/shard_map/line_scatter/pallas_call | solution.py:514
  414.0 1.8 convert_element_type.132.refs_0_
  415.8 1.3 reduce_sum.157.refs_2_
  417.2 1.7 convert_element_type.133.refs_1_
  418.9 21.8 %plane_gather.7 = (bf16[8,384,384]{2,1,0:T(8,128)(2,1)}, bf16[8,208,384]{2,1,0:T(8,128)(2,1)}, f32[8,8,128]{2,1,0:T(8,128)}) custom-call(bf16[384,384]{1,0:T(8,128)(2,1)} %convert_element_type.132.refs_0_, bf16[208,384]{1,0:T(8,128)(2,1)} %convert_element_type.133.refs_1_, f32[8,128]{1,0:T(8,128)} %reduce_sum.157.refs_2_), custom_call_target="tpu_custom_call" | custom-call | bytes 7340032 | tf_op jit(solution)/shard_map/plane_gather/pallas_call | solution.py:117
  440.7 0.8 reduce_sum.159
  441.5 2.4 slice.48
  443.9 1.0 bitcast_convert_fusion.4
  444.9 0.7 copy.82
  445.6 1.7 convert_bitcast_fusion
  447.3 2.2 copy.76
  449.5 3.1 copy.79
  452.6 1.7 convert_bitcast_fusion.1
  454.3 1.3 copy.78
  455.7 2.3 copy.81
  458.4 1.1 copy.80
  459.6 0.6 sqrt_reduce_fusion
  460.2 0.8 convert_reduce_fusion
  461.0 0.6 slice_reduce_fusion
  461.6 1.7 bitcast_convert_fusion.3
  463.3 2.8 bitcast_convert_fusion
  466.1 3.1 bitcast_convert_fusion.1
  469.2 27.4 %reduce-scatter.4.cloned.1.call-done = bf16[1,3,384,512]{3,2,1,0:T(8,128)(2,1)} async-done(((bf16[4,3,384,512]{3,2,1,0:T(8,128)(2,1)}), bf16[1,3,384,512]{3,2,1,0:T(8,128)(2,1)}) %reduce-scatter.4.cloned.1.call-update) | async-done | bytes 1179664 | tf_op jit(solution)/shard_map/reduce_scatter | solution.py:1066
  496.6 3.0 bitcast_convert_fusion.2
  (39 shorter events, 1.4 us)
Async XLA Ops:
  7.2 3.2 copy-start
  7.2 456.1 %reduce-scatter.8.cloned.1.call-start = ((), (), s32[]{:S(2)}) async-start(), calls=%async_computation.5 | async-start | bytes 5898240 | tf_op jit(solution)/shard_map/reduce_scatter | solution.py:1066
  109.1 20.5 %copy-start.2 = (bf16[1,128,1536]{2,1,0:T(8,128)(2,1)S(1)}, bf16[1,128,1536]{2,1,0:T(8,128)(2,1)}, u32[]{:S(2)}) copy-start(bf16[1,128,1536]{2,1,0:T(8,128)(2,1)} %param.13) | copy-start | bytes 1179652
  131.8 2.5 copy-start.5
  206.6 259.5 %reduce-scatter.6.cloned.1.call-start = ((), (), s32[]{:S(2)}) async-start(), calls=%async_computation.4 | async-start | bytes 5898240 | tf_op jit(solution)/shard_map/reduce_scatter | solution.py:1066
  207.4 289.3 %reduce-scatter.4.cloned.1.call-start = ((), (), s32[]{:S(2)}) async-start(), calls=%async_computation.3 | async-start | bytes 5898240 | tf_op jit(solution)/shard_map/reduce_scatter | solution.py:1066
  230.9 4.5 copy-start.6
  315.6 2.8 copy-start.7
  317.2 2.7 copy-start.4
  458.0 3.7 copy-start.3
  466.1 33.5 %copy-start.1 = (bf16[1536,384]{1,0:T(8,128)(2,1)S(1)}, bf16[1536,384]{1,0:T(8,128)(2,1)}, u32[]{:S(2)}) copy-start(bf16[1536,384]{1,0:T(8,128)(2,1)} %param.19) | copy-start | bytes 3538948
Sparse Core Ops, SparseCore 0:
  206.7 84.4 reduce-scatter.7
  293.5 114.4 reduce-scatter.5
  410.4 86.1 reduce-scatter.3
